TPU v7x, 32 devices: a whole 2x2x4 slice. The times are simulated.
32 devices in a mesh: fsdp: 4 (over y, x), ctx: 4 (over z), tp: 2 (over core).
Axes of the slice: x: 2, y: 2, z: 4, core: 2. Of those that a mesh axis runs over, the one named last changes fastest.
Arguments:
- inputs: bfloat16 [3, 1024, 4, 1024], P(None, 'ctx', 'fsdp'), may hold values from -8 to 8
- block_order: int32 [3, 4, 4], P(None, 'fsdp'), may hold values from 0 to 3, each once within a row
- first_gain: bfloat16 [1024], replicated, may hold values from 0.5 to 1.5
- first_shift: bfloat16 [1024], replicated, may hold values from -1.25 to 1.25
- second_gain: bfloat16 [1024], replicated, may hold values from 0.5 to 1.5
- second_shift: bfloat16 [1024], replicated, may hold values from -1.25 to 1.25
- qkv_weight: bfloat16 [3, 1024, 1024], P(None, ('fsdp', 'ctx'), 'tp'), may hold values from -0.1875 to 0.1875
- qkv_bias: bfloat16 [3, 1024], P(None, 'tp'), may hold values from -1.25 to 1.25
- out_weight: bfloat16 [1024, 1024], P('tp', ('fsdp', 'ctx')), may hold values from -5 to 5
- out_bias: bfloat16 [1024], replicated, may hold values from -1.25 to 1.25
- up_weight: bfloat16 [1024, 4096], P(('fsdp', 'ctx'), 'tp'), may hold values from -0.1875 to 0.1875
- up_bias: bfloat16 [4096], P('tp'), may hold values from -1.25 to 1.25
- down_weight: bfloat16 [4096, 1024], P('tp', ('fsdp', 'ctx')), may hold values from -0.09375 to 0.09375
- down_bias: bfloat16 [1024], replicated, may hold values from -1.25 to 1.25
- out_grad: bfloat16 [3, 1024, 4, 1024], P(None, 'ctx', 'fsdp'), may hold values from -8 to 8
Outputs:
- outputs: bfloat16 [3, 1024, 4, 1024], P(None, 'ctx', 'fsdp')
- input_grad: bfloat16 [3, 1024, 4, 1024], P(None, 'ctx', 'fsdp')
- first_gain_grad: float32 [1024], replicated
- first_shift_grad: float32 [1024], replicated
- second_gain_grad: float32 [1024], replicated
- second_shift_grad: float32 [1024], replicated
- qkv_weight_grad: float32 [3, 1024, 1024], P(None, ('fsdp', 'ctx'), 'tp')
- qkv_bias_grad: float32 [3, 1024], P(None, 'tp')
- out_weight_grad: float32 [1024, 1024], P('tp', ('fsdp', 'ctx'))
- out_bias_grad: float32 [1024], replicated
- up_weight_grad: float32 [1024, 4096], P(('fsdp', 'ctx'), 'tp')
- up_bias_grad: float32 [4096], P('tp')
- down_weight_grad: float32 [4096, 1024], P('tp', ('fsdp', 'ctx'))
- down_bias_grad: float32 [1024], replicated
Inputs may be any that keep to these rules, and one draw needn't show every extreme that they name: block_order[m, s, c] is the position block of the tokens at rows c * 256 to (c + 1) * 256 - 1 of sequence s of micro-batch m; each row names every block once.
All inputs are finite; a program needn't handle non-finite values.
Results may differ from a plain program's by a relative error of at most 0.014.
Values may be sent and summed in bfloat16 or wider, within the bound.
No kernel may reach another device: no remote copies, remote signals or barrier semaphores. Data moves between devices by JAX's collectives and lax.ppermute only.
A program may use at most 192 MiB of HBM per device.

v0:
```python
from functools import partial
import math

import jax
import jax.numpy as jnp
from jax import lax
from jax.sharding import PartitionSpec as P

HD = 64
ROT = 16


def norm_rows(values, scales, biases):
    centre = jnp.mean(values, axis=-1, keepdims=True)
    offset = values - centre
    spread = jnp.mean(offset * offset, axis=-1, keepdims=True)
    return offset * lax.rsqrt(spread + 1e-05) * scales + biases


def angle_tables(places, rotary):
    halves = rotary // 2
    frequency = jnp.exp(jnp.arange(halves, dtype=jnp.float32) * (-2.0 * math.log(10000.0) / rotary))
    angles = places[..., None] * frequency
    return (jnp.cos(angles)[..., None, :], jnp.sin(angles)[..., None, :])


def rotate(values, cosine_table, sine_table, rotary):
    halves = rotary // 2
    leading = values[..., :halves]
    trailing = values[..., halves:rotary]
    return jnp.concatenate(
        [
            leading * cosine_table - trailing * sine_table,
            trailing * cosine_table + leading * sine_table,
            values[..., rotary:],
        ],
        axis=-1,
    )


def rotate_back(gradient, cosine_table, sine_table, rotary):
    halves = rotary // 2
    leading = gradient[..., :halves]
    trailing = gradient[..., halves:rotary]
    return jnp.concatenate(
        [
            leading * cosine_table + trailing * sine_table,
            trailing * cosine_table - leading * sine_table,
            gradient[..., rotary:],
        ],
        axis=-1,
    )


def block_lookup(order_rows, start_row, row_count, block_rows):
    wanted = (start_row + jnp.arange(row_count, dtype=jnp.int32)) // block_rows
    match_table = wanted[:, None] == jnp.arange(order_rows.shape[1], dtype=jnp.int32)[None, :]
    return jnp.sum(jnp.where(match_table[None], order_rows[:, None, :], 0), axis=2)


def attend_piece(
    running, kv_piece, start_row, query_heads, query_blocks, order_rows, block_rows, score_scale
):
    peak_score, denominator, accumulated = running
    key_piece, value_piece = kv_piece
    row_count = key_piece.shape[0]
    shape_four = query_heads.shape
    key_heads = key_piece.reshape(row_count, shape_four[1], shape_four[2], shape_four[3])
    value_heads = value_piece.reshape(row_count, shape_four[1], shape_four[2], shape_four[3])
    key_blocks = block_lookup(order_rows, start_row, row_count, block_rows)
    allowed = (key_blocks[:, None, :] <= query_blocks[:, :, None])[:, None]
    scores = (
        jnp.einsum("bshe,rshe->shbr", query_heads, key_heads, preferred_element_type=jnp.float32)
        * score_scale
    )
    scores = jnp.where(allowed, scores, -1e30)
    new_peak = jnp.maximum(peak_score, jnp.max(scores, axis=-1))
    weights = jnp.where(allowed, jnp.exp(scores - new_peak[..., None]), 0.0)
    denominator = jnp.sum(weights, axis=-1)
    accumulated = jnp.einsum(
        "shbr,rshe->bshe",
        weights.astype(jnp.bfloat16),
        value_heads,
        preferred_element_type=jnp.float32,
    )
    return (new_peak, denominator, accumulated)


def tile_grads(
    query_heads,
    dout_heads,
    lse_rows,
    delta_rows,
    query_blocks,
    key_heads,
    value_heads,
    key_blocks,
    score_scale,
):
    scores = (
        jnp.einsum("bshe,rshe->shbr", query_heads, key_heads, preferred_element_type=jnp.float32)
        * score_scale
    )
    allowed = (key_blocks[:, None, :] <= query_blocks[:, :, None])[:, None]
    lse_table = jnp.transpose(lse_rows, (1, 2, 0))[..., None]
    delta_table = jnp.transpose(delta_rows, (1, 2, 0))[..., None]
    probability = jnp.where(allowed, jnp.exp(scores - lse_table), 0.0)
    value_grad = jnp.einsum(
        "shbr,bshe->rshe",
        probability.astype(jnp.bfloat16),
        dout_heads,
        preferred_element_type=jnp.float32,
    )
    prob_grad = jnp.einsum(
        "bshe,rshe->shbr", dout_heads, value_heads, preferred_element_type=jnp.float32
    )
    score_grad = (probability * (prob_grad - delta_table)).astype(jnp.bfloat16)
    query_grad = (
        jnp.einsum("shbr,rshe->bshe", score_grad, key_heads, preferred_element_type=jnp.float32)
        * score_scale
    )
    key_grad = (
        jnp.einsum("shbr,bshe->rshe", score_grad, query_heads, preferred_element_type=jnp.float32)
        * score_scale
    )
    return (query_grad, key_grad, value_grad)


def local(
    inputs,
    block_order,
    first_gain,
    first_shift,
    second_gain,
    second_shift,
    qkv_weight,
    qkv_bias,
    out_weight,
    out_bias,
    up_weight,
    up_bias,
    down_weight,
    down_bias,
    out_grad,
):
    micro_count, block_rows, seq_count, width = inputs.shape
    ctx_count = lax.axis_size("ctx")
    ctx_place = lax.axis_index("ctx")
    head_width = qkv_weight.shape[2]
    hidden_width = up_weight.shape[1]
    local_heads = head_width // HD
    score_scale = HD ** (-0.5)
    gain_list = tuple(
        (item.astype(jnp.float32) for item in (first_gain, first_shift, second_gain, second_shift))
    )
    qkv_shift = qkv_bias.astype(jnp.float32)
    up_shift = up_bias.astype(jnp.float32)
    end_shift = out_bias.astype(jnp.float32) + down_bias.astype(jnp.float32)
    grad_qkv = jnp.zeros((3, width, head_width), jnp.float32)
    grad_out = jnp.zeros((head_width, width), jnp.float32)
    grad_up = jnp.zeros((width, hidden_width), jnp.float32)
    grad_down = jnp.zeros((hidden_width, width), jnp.float32)
    small_list = [
        jnp.zeros((width,), jnp.float32),
        jnp.zeros((width,), jnp.float32),
        jnp.zeros((width,), jnp.float32),
        jnp.zeros((width,), jnp.float32),
        jnp.zeros((3, head_width), jnp.float32),
        jnp.zeros((width,), jnp.float32),
        jnp.zeros((hidden_width,), jnp.float32),
    ]
    outputs_list = []
    input_list = []
    for micro_index in range(micro_count):
        current = (
            lax.all_gather(qkv_weight, ("fsdp", "ctx"), axis=1, tiled=True),
            lax.all_gather(out_weight, ("fsdp", "ctx"), axis=1, tiled=True),
            lax.all_gather(up_weight, ("fsdp", "ctx"), axis=0, tiled=True),
            lax.all_gather(down_weight, ("fsdp", "ctx"), axis=1, tiled=True),
        )
        qkv_full, out_full, up_full, down_full = current
        order_rows = block_order[micro_index]
        own_blocks = jnp.sum(
            jnp.where(jnp.arange(ctx_count, dtype=jnp.int32)[None, :] == ctx_place, order_rows, 0),
            axis=1,
        )
        query_blocks = jnp.broadcast_to(own_blocks[:, None], (seq_count, block_rows))
        places = (
            own_blocks[None, :] * block_rows + jnp.arange(block_rows, dtype=jnp.int32)[:, None]
        ).astype(jnp.float32)
        cosine_table, sine_table = angle_tables(places, ROT)
        values_in = inputs[micro_index].astype(jnp.float32)
        normed_one = norm_rows(values_in, gain_list[0], gain_list[1]).astype(jnp.bfloat16)
        normed_two = norm_rows(values_in, gain_list[2], gain_list[3]).astype(jnp.bfloat16)
        projected = (
            jnp.einsum("bsd,jde->jbse", normed_one, qkv_full, preferred_element_type=jnp.float32)
            + qkv_shift[:, None, None, :]
        )
        head_views = projected.reshape(3, block_rows, seq_count, local_heads, HD)
        query_heads = rotate(head_views[0], cosine_table, sine_table, ROT).astype(jnp.bfloat16)
        key_flat = (
            rotate(head_views[1], cosine_table, sine_table, ROT)
            .astype(jnp.bfloat16)
            .reshape(block_rows, seq_count, head_width)
        )
        value_flat = projected[2].astype(jnp.bfloat16)
        attend = partial(
            attend_piece,
            query_heads=query_heads,
            query_blocks=query_blocks,
            order_rows=order_rows,
            block_rows=block_rows,
            score_scale=score_scale,
        )
        start_state = (
            jnp.full((seq_count, local_heads, block_rows), -1e30, jnp.float32),
            jnp.zeros((seq_count, local_heads, block_rows), jnp.float32),
            jnp.zeros((block_rows, seq_count, local_heads, HD), jnp.float32),
        )
        running = attend(
            start_state,
            (
                lax.all_gather(key_flat, "ctx", axis=0, tiled=True),
                lax.all_gather(value_flat, "ctx", axis=0, tiled=True),
            ),
            jnp.int32(0),
        )
        peak_score, denominator, accumulated = running
        attended = accumulated / jnp.transpose(denominator, (2, 0, 1))[..., None]
        lse_rows = jnp.transpose(peak_score + jnp.log(denominator), (2, 0, 1))
        attended_low = attended.astype(jnp.bfloat16).reshape(block_rows, seq_count, head_width)
        up_pre = (
            jnp.einsum("bsd,df->bsf", normed_two, up_full, preferred_element_type=jnp.float32)
            + up_shift
        )
        hidden = jax.nn.gelu(up_pre, approximate=False).astype(jnp.bfloat16)
        branch_part = jnp.einsum(
            "bse,ed->bsd", attended_low, out_full, preferred_element_type=jnp.float32
        ) + jnp.einsum("bsf,fd->bsd", hidden, down_full, preferred_element_type=jnp.float32)
        branch_total = lax.psum(branch_part.astype(jnp.bfloat16), "tp").astype(jnp.float32)
        outputs_list.append((values_in + branch_total + end_shift).astype(jnp.bfloat16))
        grad_rows = out_grad[micro_index]
        grad_float = grad_rows.astype(jnp.float32)
        dout_heads = (
            jnp.einsum("bsd,ed->bse", grad_rows, out_full, preferred_element_type=jnp.float32)
            .astype(jnp.bfloat16)
            .reshape(block_rows, seq_count, local_heads, HD)
        )
        hidden_grad = jnp.einsum(
            "bsd,fd->bsf", grad_rows, down_full, preferred_element_type=jnp.float32
        )
        unused_value, gelu_pull = jax.vjp(
            lambda values: jax.nn.gelu(values, approximate=False), up_pre
        )
        up_grad = gelu_pull(hidden_grad)[0].astype(jnp.bfloat16)
        grad_out = grad_out + jnp.einsum(
            "bse,bsd->ed", attended_low, grad_rows, preferred_element_type=jnp.float32
        )
        grad_down = grad_down + jnp.einsum(
            "bsf,bsd->fd", hidden, grad_rows, preferred_element_type=jnp.float32
        )
        grad_up = grad_up + jnp.einsum(
            "bsd,bsf->df", normed_two, up_grad, preferred_element_type=jnp.float32
        )
        delta_rows = jnp.sum(dout_heads.astype(jnp.float32) * attended, axis=-1)
        keys_all, values_all = (
            lax.all_gather(key_flat, "ctx", axis=0, tiled=True),
            lax.all_gather(value_flat, "ctx", axis=0, tiled=True),
        )

        def back_step(query_sum, step_item):
            piece_index, key_piece, value_piece = step_item
            key_blocks = block_lookup(order_rows, piece_index * block_rows, block_rows, block_rows)
            query_part, key_part, value_part = tile_grads(
                query_heads,
                dout_heads,
                lse_rows,
                delta_rows,
                query_blocks,
                key_piece,
                value_piece,
                key_blocks,
                score_scale,
            )
            return (query_sum + query_part, (key_part, value_part))

        query_grad, (key_parts, value_parts) = lax.scan(
            back_step,
            jnp.zeros((block_rows, seq_count, local_heads, HD), jnp.float32),
            (
                jnp.arange(ctx_count, dtype=jnp.int32),
                keys_all.reshape(ctx_count, block_rows, seq_count, local_heads, HD),
                values_all.reshape(ctx_count, block_rows, seq_count, local_heads, HD),
            ),
        )
        key_grad, value_grad = (
            lax.psum_scatter(
                key_parts.reshape(ctx_count * block_rows, seq_count, head_width).astype(
                    jnp.bfloat16
                ),
                "ctx",
                scatter_dimension=0,
                tiled=True,
            ).astype(jnp.float32),
            lax.psum_scatter(
                value_parts.reshape(ctx_count * block_rows, seq_count, head_width).astype(
                    jnp.bfloat16
                ),
                "ctx",
                scatter_dimension=0,
                tiled=True,
            ).astype(jnp.float32),
        )
        query_pre = rotate_back(query_grad, cosine_table, sine_table, ROT).reshape(
            block_rows, seq_count, head_width
        )
        key_pre = rotate_back(
            key_grad.reshape(block_rows, seq_count, local_heads, HD), cosine_table, sine_table, ROT
        ).reshape(block_rows, seq_count, head_width)
        stacked = jnp.stack([query_pre, key_pre, value_grad]).astype(jnp.bfloat16)
        grad_qkv = grad_qkv + jnp.einsum(
            "bsd,jbse->jde", normed_one, stacked, preferred_element_type=jnp.float32
        )
        normed_grad_one = jnp.einsum(
            "jbse,jde->bsd", stacked, qkv_full, preferred_element_type=jnp.float32
        )
        normed_grad_two = jnp.einsum(
            "bsf,df->bsd", up_grad, up_full, preferred_element_type=jnp.float32
        )
        normed_grad_one, normed_grad_two = (
            lax.psum(normed_grad_one.astype(jnp.bfloat16), "tp").astype(jnp.float32),
            lax.psum(normed_grad_two.astype(jnp.bfloat16), "tp").astype(jnp.float32),
        )
        unused_one, norm_pull_one = jax.vjp(norm_rows, values_in, gain_list[0], gain_list[1])
        input_one, gain_one, shift_one = norm_pull_one(normed_grad_one)
        unused_two, norm_pull_two = jax.vjp(norm_rows, values_in, gain_list[2], gain_list[3])
        input_two, gain_two, shift_two = norm_pull_two(normed_grad_two)
        input_list.append((grad_float + input_one + input_two).astype(jnp.bfloat16))
        small_list = [
            small_list[0] + gain_one,
            small_list[1] + shift_one,
            small_list[2] + gain_two,
            small_list[3] + shift_two,
            small_list[4] + jnp.sum(stacked.astype(jnp.float32), axis=(1, 2)),
            small_list[5] + jnp.sum(grad_float, axis=(0, 1)),
            small_list[6] + jnp.sum(up_grad.astype(jnp.float32), axis=(0, 1)),
        ]
    weight_sums = (
        lax.psum_scatter(grad_qkv, ("fsdp", "ctx"), scatter_dimension=1, tiled=True),
        lax.psum_scatter(grad_out, ("fsdp", "ctx"), scatter_dimension=1, tiled=True),
        lax.psum_scatter(grad_up, ("fsdp", "ctx"), scatter_dimension=0, tiled=True),
        lax.psum_scatter(grad_down, ("fsdp", "ctx"), scatter_dimension=1, tiled=True),
    )
    small_sums = lax.psum(
        (
            small_list[0],
            small_list[1],
            small_list[2],
            small_list[3],
            small_list[4],
            small_list[5],
            small_list[6],
        ),
        ("fsdp", "ctx"),
    )
    return (
        jnp.stack(outputs_list),
        jnp.stack(input_list),
        small_sums[0],
        small_sums[1],
        small_sums[2],
        small_sums[3],
        weight_sums[0],
        small_sums[4],
        weight_sums[1],
        small_sums[5],
        weight_sums[2],
        small_sums[6],
        weight_sums[3],
        small_sums[5],
    )


def solution(mesh):
    placed = (
        P(None, "ctx", "fsdp", None),
        P(None, "fsdp", None),
        P(),
        P(),
        P(),
        P(),
        P(None, ("fsdp", "ctx"), "tp"),
        P(None, "tp"),
        P("tp", ("fsdp", "ctx")),
        P(),
        P(("fsdp", "ctx"), "tp"),
        P("tp"),
        P("tp", ("fsdp", "ctx")),
        P(),
        P(None, "ctx", "fsdp", None),
    )
    return jax.shard_map(
        local,
        mesh=mesh,
        in_specs=placed,
        out_specs=(
            P(None, "ctx", "fsdp", None),
            P(None, "ctx", "fsdp", None),
            P(),
            P(),
            P(),
            P(),
            P(None, ("fsdp", "ctx"), "tp"),
            P(None, "tp"),
            P("tp", ("fsdp", "ctx")),
            P(),
            P(("fsdp", "ctx"), "tp"),
            P("tp"),
            P("tp", ("fsdp", "ctx")),
            P(),
        ),
        check_vma=False,
    )
```

profile of v0, /device:TPU:0, one launch (start us, length us, event | category | flops | bytes accessed | tf_op | source)
XLA Modules:
  0.0 1397.2 jit_solution(3652406772502838443)
XLA Ops:
  17.3 63.9 %all-gather.14.cloned.1.call-done = bf16[3,1024,512]{2,1,0:T(8,128)(2,1)} async-done(((bf16[3,64,512]{2,1,0:T(8,128)(2,1)}), bf16[3,1024,512]{2,1,0:T(8,128)(2,1)}) %all-gather.14.cloned.1.call-update) | async-done | bytes 3145744 | tf_op jit(solution)/shard_map/all_gather | solution.py:176
  116.1 22.4 %all-gather.18.cloned.1.call-done = bf16[512,1024]{0,1:T(8,128)(2,1)} async-done(((bf16[512,64]{0,1:T(8,128)(2,1)}), bf16[512,1024]{0,1:T(8,128)(2,1)}) %all-gather.18.cloned.1.call-update) | async-done | bytes 1048592 | tf_op jit(solution)/shard_map/all_gather | solution.py:177
  149.7 19.4 %all-gather.24.cloned.1.call-done = bf16[1024,1,512]{0,2,1:T(8,128)(2,1)} async-done(((bf16[256,1,512]{0,2,1:T(8,128)(2,1)}), bf16[1024,1,512]{0,2,1:T(8,128)(2,1)}) %all-gather.24.cloned.1.call-update) | async-done | bytes 1048592 | tf_op jit(solution)/shard_map/all_gather | solution.py:223
  177.0 19.8 %all-gather.30.cloned.1.call-done = bf16[1,1024,1,512]{3,1,0,2:T(8,128)(2,1)} async-done(((bf16[1,256,1,512]{3,1,0,2:T(8,128)(2,1)}), bf16[1,1024,1,512]{3,1,0,2:T(8,128)(2,1)}) %all-gather.30.cloned.1.call-update) | async-done | bytes 1048592 | tf_op jit(solution)/shard_map/all_gather | solution.py:224
  203.0 6.2 multiply_reduce_fusion.1
  211.5 46.7 %while.52 = (s32[]{:T(128)}, f32[256,1,8,64]{0,3,2,1:T(8,128)}, bf16[4,256,1,8,64]{1,4,3,2,0:T(8,128)(2,1)}, bf16[4,256,1,8,64]{1,4,3,2,0:T(8,128)(2,1)}, bf16[4...) while((s32[]{:T(128)}, f32[256,1,8,64]{0,3,2,1:T(8,128)}, ...), condition=%wide.region_36.37_spmd.clone, body=%wide.region_34.36_spmd.clone.sunk | while | flops 339745792 | bytes 15556187 | solution.py:287
  275.9 6.0 multiply_reduce_fusion.2
  284.1 46.0 %while.51 = (s32[]{:T(128)}, f32[256,1,8,64]{0,3,2,1:T(8,128)}, bf16[4,256,1,8,64]{1,4,3,2,0:T(8,128)(2,1)}, bf16[4,256,1,8,64]{1,4,3,2,0:T(8,128)(2,1)}, bf16[4...) while((s32[]{:T(128)}, f32[256,1,8,64]{0,3,2,1:T(8,128)}, ...), condition=%wide.region_24.25_spmd.clone, body=%wide.region_22.24_spmd.clone.sunk | while | flops 339745792 | bytes 14441715 | solution.py:287
  347.9 6.0 multiply_reduce_fusion
  356.2 41.7 %while.53 = (s32[]{:T(128)}, f32[256,1,8,64]{0,3,2,1:T(8,128)}, bf16[4,256,1,8,64]{1,4,3,2,0:T(8,128)(2,1)}, bf16[4,256,1,8,64]{1,4,3,2,0:T(8,128)(2,1)}, bf16[4...) while((s32[]{:T(128)}, f32[256,1,8,64]{0,3,2,1:T(8,128)}, ...), condition=%wide.region_48.49_spmd.clone, body=%wide.region_46.48_spmd.clone.sunk | while | flops 339745792 | bytes 14441715 | solution.py:287
  422.8 9.1 multiply_convert_fusion.2
  431.9 7.5 multiply_convert_fusion.1
  439.4 7.9 multiply_convert_fusion
  447.3 22.7 %all-gather.22.cloned.1.call-done = bf16[2048,1024]{0,1:T(8,128)(2,1)} async-done(((bf16[2048,64]{0,1:T(8,128)(2,1)}), bf16[2048,1024]{0,1:T(8,128)(2,1)}) %all-gather.22.cloned.1.call-update) | async-done | bytes 4194320 | tf_op jit(solution)/shard_map/all_gather | solution.py:179
  501.5 24.7 %reduce-scatter.10.cloned.1.call-done = bf16[256,1,512]{0,2,1:T(8,128)(2,1)} async-done(((bf16[1024,1,512]{0,2,1:T(8,128)(2,1)}), bf16[256,1,512]{0,2,1:T(8,128)(2,1)}) %reduce-scatter.10.cloned.1.call-update) | async-done | bytes 262160 | tf_op jit(solution)/shard_map/reduce_scatter | solution.py:297
  529.6 24.7 %reduce-scatter.18.cloned.1.call-done = bf16[256,1,512]{0,2,1:T(8,128)(2,1)} async-done(((bf16[1024,1,512]{0,2,1:T(8,128)(2,1)}), bf16[256,1,512]{0,2,1:T(8,128)(2,1)}) %reduce-scatter.18.cloned.1.call-update) | async-done | bytes 262160 | tf_op jit(solution)/shard_map/reduce_scatter | solution.py:297
  586.3 24.0 %reduce-scatter.16.cloned.1.call-done = bf16[256,1,512]{2,0,1:T(8,128)(2,1)} async-done(((bf16[1024,1,512]{2,0,1:T(8,128)(2,1)}), bf16[256,1,512]{2,0,1:T(8,128)(2,1)}) %reduce-scatter.16.cloned.1.call-update) | async-done | bytes 262160 | tf_op jit(solution)/shard_map/reduce_scatter | solution.py:305
  614.3 24.1 %reduce-scatter.20.cloned.1.call-done = bf16[256,1,512]{2,0,1:T(8,128)(2,1)} async-done(((bf16[1024,1,512]{2,0,1:T(8,128)(2,1)}), bf16[256,1,512]{2,0,1:T(8,128)(2,1)}) %reduce-scatter.20.cloned.1.call-update) | async-done | bytes 262160 | tf_op jit(solution)/shard_map/reduce_scatter | solution.py:305
  651.4 9.5 copy.249
  705.6 79.5 %all-reduce.1 = (f32[1024]{0:T(1024)}, f32[1024]{0:T(1024)}, f32[1024]{0:T(1024)}, f32[1024]{0:T(1024)}, f32[3,512]{1,0:T(4,128)}, /*index=5*/f32[1024]{0:T(1024)S(1)}, f32[2048]{0:T(1024)}) all-reduce(f32[1024]{0:T(1024)S(1)} %add_add_fusion.15, ...), channel_id=1, replica_groups=mesh['fsdp'=4,'ctx'=4,'tp'=2] {'fsdp','ctx'}, use_global_device_ids=true, to_apply=%region_60.61 | all-reduce | flops 8704 | bytes 69632 | tf_op jit(solution)/shard_map/psum | solution.py:354
  792.1 146.4 %all-reduce.6.cloned.1.call-done = f32[3,1024,512]{2,0,1:T(4,128)} async-done(((f32[3,1024,512]{2,0,1:T(4,128)}), f32[3,1024,512]{2,0,1:T(4,128)}) %all-reduce.6.cloned.1.call-update) | async-done | bytes 6291472
  940.5 84.1 %reduce-scatter.22.cloned.1.call-done = f32[512,64]{0,1:T(8,128)} async-done(((f32[512,1024]{0,1:T(8,128)}), f32[512,64]{0,1:T(8,128)}) %reduce-scatter.22.cloned.1.call-update) | async-done | bytes 131088 | tf_op jit(solution)/shard_map/reduce_scatter | solution.py:350
  1024.6 181.9 %reduce-scatter.24.cloned.1.call-done = f32[64,2048]{1,0:T(8,128)} async-done(((f32[1024,2048]{1,0:T(8,128)}), f32[64,2048]{1,0:T(8,128)}) %reduce-scatter.24.cloned.1.call-update) | async-done | bytes 524304 | tf_op jit(solution)/shard_map/reduce_scatter | solution.py:351
  1206.5 182.8 %reduce-scatter.26.cloned.1.call-done = f32[2048,64]{0,1:T(8,128)} async-done(((f32[2048,1024]{0,1:T(8,128)}), f32[2048,64]{0,1:T(8,128)}) %reduce-scatter.26.cloned.1.call-update) | async-done | bytes 524304 | tf_op jit(solution)/shard_map/reduce_scatter | solution.py:352
  (671 shorter events, 396.7 us)
Async XLA Ops:
  7.2 74.1 %all-gather.14.cloned.1.call-start = ((), (), s32[]{:S(2)}) async-start(), calls=%async_computation.9 | async-start | bytes 3342336 | tf_op jit(solution)/shard_map/all_gather | solution.py:176
  7.9 130.6 %all-gather.18.cloned.1.call-start = ((), (), s32[]{:S(2)}) async-start(), calls=%async_computation.11 | async-start | bytes 1114112 | tf_op jit(solution)/shard_map/all_gather | solution.py:177
  8.7 160.4 %all-gather.24.cloned.1.call-start = ((), (), s32[]{:S(2)}) async-start(), calls=%async_computation.14 | async-start | bytes 1310720 | tf_op jit(solution)/shard_map/all_gather | solution.py:223
  17.3 89.5 %copy-start.65 = (f32[256,8]{0,1:T(8,128)}, f32[256,8]{0,1:T(8,128)S(1)}, u32[]{:S(2)}) copy-start(f32[256,8]{0,1:T(8,128)S(1)} %get-tuple-element.1084) | copy-start | bytes 24580
  17.3 89.5 %copy-start.67 = (f32[256,8]{0,1:T(8,128)}, f32[256,8]{0,1:T(8,128)S(1)}, u32[]{:S(2)}) copy-start(f32[256,8]{0,1:T(8,128)S(1)} %get-tuple-element.1085) | copy-start | bytes 24580
  87.2 109.6 %all-gather.30.cloned.1.call-start = ((), (), s32[]{:S(2)}) async-start(), calls=%async_computation.26 | async-start | bytes 1310720 | tf_op jit(solution)/shard_map/all_gather | solution.py:224
  89.1 172.7 %all-gather.16.cloned.1.call-start = ((), (), s32[]{:S(2)}) async-start(), calls=%async_computation.10 | async-start | bytes 1310720 | tf_op jit(solution)/shard_map/all_gather | solution.py:223
  98.4 166.4 %all-gather.28.cloned.1.call-start = ((), (), s32[]{:S(2)}) async-start(), calls=%async_computation.25 | async-start | bytes 1310720 | tf_op jit(solution)/shard_map/all_gather | solution.py:224
  100.3 233.4 %all-gather.26.cloned.1.call-start = ((), (), s32[]{:S(2)}) async-start(), calls=%async_computation.15 | async-start | bytes 1310720 | tf_op jit(solution)/shard_map/all_gather | solution.py:223
  108.5 228.3 %all-gather.32.cloned.1.call-start = ((), (), s32[]{:S(2)}) async-start(), calls=%async_computation.27 | async-start | bytes 1310720 | tf_op jit(solution)/shard_map/all_gather | solution.py:224
  110.3 312.4 %all-gather.20.cloned.1.call-start = ((), (), s32[]{:S(2)}) async-start(), calls=%async_computation.12 | async-start | bytes 4456448 | tf_op jit(solution)/shard_map/all_gather | solution.py:178
  111.1 358.9 %all-gather.22.cloned.1.call-start = ((), (), s32[]{:S(2)}) async-start(), calls=%async_computation.13 | async-start | bytes 4456448 | tf_op jit(solution)/shard_map/all_gather | solution.py:179
  111.7 386.4 %reduce-scatter.14.cloned.1.call-start = ((), (), s32[]{:S(2)}) async-start(), calls=%async_computation.18 | async-start | bytes 1310720 | tf_op jit(solution)/shard_map/reduce_scatter | solution.py:297
  275.2 250.9 %reduce-scatter.10.cloned.1.call-start = ((), (), s32[]{:S(2)}) async-start(), calls=%async_computation.16 | async-start | bytes 1310720 | tf_op jit(solution)/shard_map/reduce_scatter | solution.py:297
  347.2 207.1 %reduce-scatter.18.cloned.1.call-start = ((), (), s32[]{:S(2)}) async-start(), calls=%async_computation.20 | async-start | bytes 1310720 | tf_op jit(solution)/shard_map/reduce_scatter | solution.py:297
  401.5 180.8 %reduce-scatter.12.cloned.1.call-start = ((), (), s32[]{:S(2)}) async-start(), calls=%async_computation.17 | async-start | bytes 1310720 | tf_op jit(solution)/shard_map/reduce_scatter | solution.py:305
  405.9 204.4 %reduce-scatter.16.cloned.1.call-start = ((), (), s32[]{:S(2)}) async-start(), calls=%async_computation.19 | async-start | bytes 1310720 | tf_op jit(solution)/shard_map/reduce_scatter | solution.py:305
  410.3 228.1 %reduce-scatter.20.cloned.1.call-start = ((), (), s32[]{:S(2)}) async-start(), calls=%async_computation.21 | async-start | bytes 1310720 | tf_op jit(solution)/shard_map/reduce_scatter | solution.py:305
  422.7 275.6 %all-reduce.8.cloned.1.call-start = ((), (), s32[]{:S(2)}) async-start(), calls=%async_computation.29 | async-start | bytes 9437184 | tf_op jit(solution)/shard_map/psum | solution.py:240
  642.4 296.1 %all-reduce.6.cloned.1.call-start = ((), (), s32[]{:S(2)}) async-start(), calls=%async_computation.28 | async-start | bytes 16777216
  660.9 363.7 %reduce-scatter.22.cloned.1.call-start = ((), (), s32[]{:S(2)}) async-start(), calls=%async_computation.22 | async-start | bytes 2228224 | tf_op jit(solution)/shard_map/reduce_scatter | solution.py:350
  665.3 541.2 %reduce-scatter.24.cloned.1.call-start = ((), (), s32[]{:S(2)}) async-start(), calls=%async_computation.23 | async-start | bytes 8912896 | tf_op jit(solution)/shard_map/reduce_scatter | solution.py:351
  674.6 714.7 %reduce-scatter.26.cloned.1.call-start = ((), (), s32[]{:S(2)}) async-start(), calls=%async_computation.24 | async-start | bytes 8912896 | tf_op jit(solution)/shard_map/reduce_scatter | solution.py:352
  785.2 604.1 %copy-start.109 = (f32[1024]{0:T(1024)}, f32[1024]{0:T(1024)S(1)}, u32[]{:S(2)}) copy-start(f32[1024]{0:T(1024)S(1)} %get-tuple-element.1516) | copy-start | bytes 12292
  (150 other events, 1460.9 us)
Sparse Core Ops, SparseCore 0:
  10.8 70.3 all-gather.13
  84.0 54.4 all-gather.17
  140.1 28.9 all-gather.23
  170.5 26.2 all-gather.29
  198.2 29.7 all-gather.15
  229.4 26.2 all-gather.27
  257.2 29.6 all-gather.25
  288.5 26.2 all-gather.31
  317.6 75.2 all-gather.19
  395.5 74.5 all-gather.21
  472.3 25.7 reduce-scatter.13
  500.3 25.7 reduce-scatter.9
  528.4 25.7 reduce-scatter.17
  556.5 25.7 reduce-scatter.11
  584.5 25.7 reduce-scatter.15
  612.6 25.7 reduce-scatter.19
  642.5 29.5 all-reduce.7
  679.0 259.4 all-reduce.5
  941.5 83.0 reduce-scatter.21
  1027.4 179.0 reduce-scatter.23
  1209.5 179.8 reduce-scatter.25
where the time goes:
time: 1410 us; the launch traced here: 1400 us
  waiting for transfers between devices  847 us (60%)
  matrix products  238 us (17%)
  local copies, waits for them, and re-layouts  137 us (10%)
  blocking collectives  79.5 us (6%)
  other arithmetic  67.5 us (5%)
  between operations  19.2 us (1%)
    reduce_scatter x1, waiting for transfers between devices, local(): lax.psum_scatter(grad_down, ('fsdp', 'ctx'), scatter_dimension=1, tiled=T...  183 us
    reduce_scatter x1, waiting for transfers between devices, local(): lax.psum_scatter(grad_up, ('fsdp', 'ctx'), scatter_dimension=0, tiled=True)  182 us
    unnamed x22, waiting for transfers between devices  149 us
    reduce_scatter x1, waiting for transfers between devices, local(): lax.psum_scatter(grad_out, ('fsdp', 'ctx'), scatter_dimension=1, tiled=True)  84.1 us
    psum x1, blocking collectives, local(): lax.psum((small_list[0], small_list[1], small_list[2], small_list[3], sma...  79.5 us
    all_gather x1, waiting for transfers between devices, local(): lax.all_gather(qkv_weight, ('fsdp', 'ctx'), axis=1, tiled=True)  63.9 us
    reduce_scatter x3, waiting for transfers between devices, local(): lax.psum_scatter(value_parts.reshape(ctx_count * block_rows, seq_count, h...  50.8 us
    reduce_scatter x3, waiting for transfers between devices, local(): lax.psum_scatter(key_parts.reshape(ctx_count * block_rows, seq_count, hea...  50 us
  transfers between devices with their start and end apart: 21, of which 15 were waited for; matrix products, arithmetic and copies ran while one was open for 31% of the time, Pallas kernels for 0%

commit v1 on v0

v1 whole, which is shorter than its diff:
```python
import math

import jax
import jax.numpy as jnp
from jax import lax
from jax.experimental import pallas as pl
from jax.experimental.pallas import tpu as pltpu
from jax.sharding import PartitionSpec as P

HD = 64
ROT = 16
LANES = 128
F32 = jnp.float32
BF16 = jnp.bfloat16
VMEM_BYTES = 56 * 1024 * 1024


def rotate_ring(value, axis, step):
    size = lax.axis_size(axis)
    return lax.ppermute(value, axis, [(i, (i + step) % size) for i in range(size)])


def swap_bit(value, axis, bit):
    size = lax.axis_size(axis)
    return lax.ppermute(value, axis, [(i, i ^ bit) for i in range(size)])


def place(buffer, value, starts):
    return lax.dynamic_update_slice(buffer, value, starts)


def gather_rows(shard, bit_orders):
    rows, width = shard.shape
    fsdp, ctx = lax.axis_size("fsdp"), lax.axis_size("ctx")
    f, z = lax.axis_index("fsdp"), lax.axis_index("ctx")
    column = jnp.zeros((ctx * rows, width), shard.dtype)
    column = place(column, shard, (z * rows, 0))
    for step in range(1, ctx):
        got = rotate_ring(shard, "ctx", step)
        column = place(column, got, (((z - step) % ctx) * rows, 0))
    part = width // len(bit_orders)
    whole = jnp.zeros((fsdp * ctx * rows, width), shard.dtype)
    for index, bits in enumerate(bit_orders):
        pieces = {0: column[:, index * part : (index + 1) * part]}
        for bit in bits:
            for offset in list(pieces):
                pieces[offset | bit] = swap_bit(pieces[offset], "fsdp", bit)
        for offset, piece in pieces.items():
            whole = place(whole, piece, ((f ^ offset) * (ctx * rows), index * part))
    return whole


def scatter_rows(partial, bits):
    fsdp, ctx = lax.axis_size("fsdp"), lax.axis_size("ctx")
    f, z = lax.axis_index("fsdp"), lax.axis_index("ctx")
    rows, width = partial.shape[0] // (fsdp * ctx), partial.shape[1]
    block = ctx * rows
    sums = {
        offset: lax.dynamic_slice(partial, ((f ^ offset) * block, 0), (block, width))
        for offset in range(fsdp)
    }
    for bit in reversed(bits):
        for offset in [key for key in sums if key & bit]:
            got = swap_bit(sums.pop(offset).astype(BF16), "fsdp", bit)
            sums[offset ^ bit] = sums[offset ^ bit] + got.astype(F32)
    mine = sums[0]
    total = lax.dynamic_slice(mine, (z * rows, 0), (rows, width))
    for step in range(1, ctx):
        piece = lax.dynamic_slice(mine, (((z + step) % ctx) * rows, 0), (rows, width))
        total = total + rotate_ring(piece.astype(BF16), "ctx", step).astype(F32)
    return total


def sum_small(value):
    for axis in ("fsdp", "ctx"):
        bit = 1
        while bit < lax.axis_size(axis):
            value = value + swap_bit(value, axis, bit)
            bit *= 2
    return value


def other_core(value):
    return lax.ppermute(value, "tp", [(0, 1), (1, 0)])


def turn(values, cosine, sine):
    lane = lax.broadcasted_iota(jnp.int32, values.shape, 1) % HD
    ahead = pltpu.roll(values, LANES - ROT // 2, 1)
    behind = pltpu.roll(values, ROT // 2, 1)
    return values * cosine + jnp.where(lane < ROT // 2, -ahead, behind) * sine


def project_kernel(order_ref, normed_ref, grad_ref, weight_ref, bias_ref, table_ref, out_ref):
    width = 3 * LANES
    weight = weight_ref[...]
    pre = jnp.dot(normed_ref[...], weight[:, :width], preferred_element_type=F32) + bias_ref[0]
    cosine, sine = table_ref[0], table_ref[1]
    out_ref[0, 0, :, :LANES] = turn(pre[:, :LANES], cosine, sine).astype(BF16)
    out_ref[0, 0, :, LANES : 2 * LANES] = turn(pre[:, LANES : 2 * LANES], cosine, sine).astype(BF16)
    out_ref[0, 0, :, 2 * LANES : width] = pre[:, 2 * LANES :].astype(BF16)
    back = jnp.dot(grad_ref[...], weight[:, width:], preferred_element_type=F32)
    out_ref[0, 0, :, width:] = back.astype(BF16)


def project(own_order, normed, grad_rows, weight, bias, table, block_rows):
    tokens, width = normed.shape
    micro = tokens // block_rows
    groups = weight.shape[1] // (4 * LANES)
    return pl.pallas_call(
        project_kernel,
        out_shape=jax.ShapeDtypeStruct((groups, micro, block_rows, 4 * LANES), BF16),
        grid_spec=pltpu.PrefetchScalarGridSpec(
            num_scalar_prefetch=1,
            grid=(groups, micro),
            in_specs=[
                pl.BlockSpec((block_rows, width), lambda g, m, order: (m, 0)),
                pl.BlockSpec((block_rows, width), lambda g, m, order: (m, 0)),
                pl.BlockSpec((width, 4 * LANES), lambda g, m, order: (0, g)),
                pl.BlockSpec((1, 1, 3 * LANES), lambda g, m, order: (g, 0, 0)),
                pl.BlockSpec((2, block_rows, LANES), lambda g, m, order: (0, order[m], 0)),
            ],
            out_specs=pl.BlockSpec(
                (1, 1, block_rows, 4 * LANES), lambda g, m, order: (g, m, 0, 0)
            ),
        ),
        compiler_params=pltpu.CompilerParams(vmem_limit_bytes=VMEM_BYTES),
        cost_estimate=pl.CostEstimate(
            flops=2 * tokens * width * weight.shape[1],
            bytes_accessed=2 * (weight.size + groups * tokens * 4 * LANES + 2 * normed.size),
            transcendentals=0,
        ),
    )(own_order, normed, grad_rows, weight, bias, table)


def attend_kernel(blocks, block_rows, scale, rank_ref, table_ref, *refs):
    chunk_refs, out_refs = refs[:blocks], refs[blocks : 2 * blocks]
    q_s, k_s, v_s, d_s, kt_s, vt_s, ot_s, qt_s, dk_s, dv_s = refs[2 * blocks :]
    for index in range(blocks):
        rows = pl.ds(pl.multiple_of(rank_ref[index] * block_rows, block_rows), block_rows)
        q_s[rows, :] = chunk_refs[index][:, :LANES]
        k_s[rows, :] = chunk_refs[index][:, LANES : 2 * LANES]
        v_s[rows, :] = chunk_refs[index][:, 2 * LANES : 3 * LANES]
        d_s[rows, :] = chunk_refs[index][:, 3 * LANES :]
    kt_s[...] = k_s[...].T
    vt_s[...] = v_s[...].T
    dk_s[...] = jnp.zeros_like(dk_s)
    dv_s[...] = jnp.zeros_like(dv_s)
    lane = lax.broadcasted_iota(jnp.int32, (block_rows, LANES), 1)
    matmul = lambda a, b: jnp.dot(a, b, preferred_element_type=F32)
    outer = lambda a, b: lax.dot_general(a, b, (((1,), (1,)), ((), ())), preferred_element_type=F32)
    for rank in range(blocks):
        rows = slice(rank * block_rows, (rank + 1) * block_rows)
        keys = slice(0, (rank + 1) * block_rows)
        for head in range(LANES // HD):
            inside = (lane // HD) == head
            heads = slice(head * HD, (head + 1) * HD)
            q_h = jnp.where(inside, q_s[rows, :], 0).astype(BF16)
            d_h = jnp.where(inside, d_s[rows, :], 0).astype(BF16)
            scores = outer(k_s[keys, :], q_h) * scale
            weights = jnp.exp(scores - jnp.max(scores, axis=0, keepdims=True))
            weights = weights * (1.0 / jnp.sum(weights, axis=0, keepdims=True))
            low = weights.astype(BF16)
            ot_s[heads, rows] = matmul(vt_s[heads, keys], low)
            dv_s[keys, :] += matmul(low, d_h)
            slope = outer(v_s[keys, :], d_h)
            delta = jnp.sum(weights * slope, axis=0, keepdims=True)
            slope = (weights * (slope - delta)).astype(BF16)
            qt_s[heads, rows] = matmul(kt_s[heads, keys], slope)
            dk_s[keys, :] += matmul(slope, q_h)
    for index in range(blocks):
        rows = pl.ds(pl.multiple_of(rank_ref[index] * block_rows, block_rows), block_rows)
        cosine, sine = table_ref[0, rows, :], -table_ref[1, rows, :]
        out_refs[index][:, :LANES] = ot_s[:, rows].T.astype(BF16)
        out_refs[index][:, LANES : 2 * LANES] = turn(qt_s[:, rows].T * scale, cosine, sine).astype(BF16)
        out_refs[index][:, 2 * LANES : 3 * LANES] = turn(dk_s[rows, :] * scale, cosine, sine).astype(BF16)
        out_refs[index][:, 3 * LANES :] = dv_s[rows, :].astype(BF16)


def attend(ranks, table, chunks):
    blocks, block_rows = len(chunks), chunks[0].shape[0]
    length = blocks * block_rows
    spec = pl.BlockSpec(memory_space=pltpu.VMEM)
    pairs = blocks * (blocks + 1) // 2 * block_rows * block_rows
    return pl.pallas_call(
        lambda *refs: attend_kernel(blocks, block_rows, HD ** (-0.5), *refs),
        out_shape=[jax.ShapeDtypeStruct(chunk.shape, BF16) for chunk in chunks],
        in_specs=[pl.BlockSpec(memory_space=pltpu.SMEM), spec] + [spec] * blocks,
        out_specs=[spec] * blocks,
        scratch_shapes=[pltpu.VMEM((length, LANES), BF16)] * 4
        + [pltpu.VMEM((LANES, length), BF16)] * 2
        + [pltpu.VMEM((LANES, length), F32)] * 2
        + [pltpu.VMEM((length, LANES), F32)] * 2,
        compiler_params=pltpu.CompilerParams(vmem_limit_bytes=VMEM_BYTES),
        cost_estimate=pl.CostEstimate(
            flops=pairs * 2 * 2 * LANES * 7,
            bytes_accessed=length * 4 * LANES * 4,
            transcendentals=pairs * 2,
        ),
    )(ranks, table, *chunks)


def exchange_attention(packed, order, table):
    groups, micro, block_rows, width = packed.shape
    z = lax.axis_index("ctx")
    results = []
    for m in range(micro):
        chunks = []
        for step in range(groups):
            chunk = lax.dynamic_slice(packed, ((z + step) % groups, m, 0, 0), (1, 1, block_rows, width))
            chunk = chunk.reshape(block_rows, width)
            chunks.append(chunk if step == 0 else rotate_ring(chunk, "ctx", step))
        ranks = jnp.stack([order[m, (z - step) % groups] for step in range(groups)])
        outs = attend(ranks, table, chunks)
        back = jnp.zeros((groups, block_rows, width), BF16)
        for step in range(groups):
            got = outs[step] if step == 0 else rotate_ring(outs[step], "ctx", groups - step)
            back = place(back, got[None], ((z + step) % groups, 0, 0))
        results.append(back)
    return results


def gathered_attention(packed, order, table):
    groups, micro, block_rows, width = packed.shape
    ctx, z = lax.axis_size("ctx"), lax.axis_index("ctx")
    heads = groups * LANES // HD
    scale = HD ** (-0.5)

    def split(array):
        lead = array.shape[:-2]
        array = array.reshape(*lead, block_rows, LANES // HD, HD)
        array = jnp.moveaxis(array, 0, -3)
        return array.reshape(*array.shape[:-3], heads, HD)

    results = []
    for m in range(micro):
        own = order[m, z]
        parts = packed[:, m].reshape(groups, block_rows, 4, LANES)
        queries, keys, values, douts = (split(parts[:, :, i]) for i in range(4))
        all_keys = lax.all_gather(keys, "ctx", axis=0)
        all_values = lax.all_gather(values, "ctx", axis=0)
        allowed = order[m] <= own

        def peak_step(state, item):
            key, value, ok = item
            peak, total, sums = state
            scores = jnp.einsum("bhe,rhe->hbr", queries, key, preferred_element_type=F32) * scale
            scores = jnp.where(ok, scores, -1e30)
            new = jnp.maximum(peak, jnp.max(scores, axis=-1))
            weights = jnp.where(ok, jnp.exp(scores - new[..., None]), 0.0)
            keep = jnp.exp(peak - new)
            part = jnp.einsum("hbr,rhe->hbe", weights.astype(BF16), value, preferred_element_type=F32)
            return (new, total * keep + jnp.sum(weights, axis=-1), sums * keep[..., None] + part), None

        start = (
            jnp.full((heads, block_rows), -1e30, F32),
            jnp.zeros((heads, block_rows), F32),
            jnp.zeros((heads, block_rows, HD), F32),
        )
        (peak, total, sums), _ = lax.scan(peak_step, start, (all_keys, all_values, allowed))
        attended = jnp.transpose(sums / total[..., None], (1, 0, 2))
        level = peak + jnp.log(total)
        delta = jnp.transpose(jnp.sum(douts.astype(F32) * attended, axis=-1))

        def back_step(query_sum, item):
            key, value, ok = item
            scores = jnp.einsum("bhe,rhe->hbr", queries, key, preferred_element_type=F32) * scale
            weights = jnp.where(ok, jnp.exp(scores - level[..., None]), 0.0)
            value_grad = jnp.einsum("hbr,bhe->rhe", weights.astype(BF16), douts, preferred_element_type=F32)
            slope = jnp.einsum("bhe,rhe->hbr", douts, value, preferred_element_type=F32)
            slope = (weights * (slope - delta[..., None])).astype(BF16)
            query_part = jnp.einsum("hbr,rhe->bhe", slope, key, preferred_element_type=F32) * scale
            key_grad = jnp.einsum("hbr,bhe->rhe", slope, queries, preferred_element_type=F32) * scale
            return query_sum + query_part, (key_grad.astype(BF16), value_grad.astype(BF16))

        query_grad, (key_grads, value_grads) = lax.scan(
            back_step, jnp.zeros(queries.shape, F32), (all_keys, all_values, allowed)
        )
        key_grad = lax.psum_scatter(key_grads, "ctx", scatter_dimension=0).astype(F32)
        value_grad = lax.psum_scatter(value_grads, "ctx", scatter_dimension=0)
        rows = lax.dynamic_slice(table, (0, own * block_rows, 0), (2, block_rows, LANES))

        def join(array):
            array = array.reshape(block_rows, groups, LANES)
            return jnp.transpose(array, (1, 0, 2))

        def unturn(array):
            half = ROT // 2
            cosine, sine = rows[0, :, :half][:, None], rows[1, :, :half][:, None]
            first, second = array[..., :half], array[..., half:ROT]
            return jnp.concatenate(
                [first * cosine + second * sine, second * cosine - first * sine, array[..., ROT:]], axis=-1
            )

        results.append(
            jnp.concatenate(
                [
                    join(attended.astype(BF16)),
                    join(unturn(query_grad).astype(BF16)),
                    join(unturn(key_grad).astype(BF16)),
                    join(value_grad.astype(BF16)),
                ],
                axis=-1,
            )
        )
    return results


def across(lhs, rhs):
    return lax.dot_general(lhs, rhs, (((0,), (0,)), ((), ())), preferred_element_type=F32)


def against(lhs, rhs):
    return lax.dot_general(lhs, rhs, (((1,), (1,)), ((), ())), preferred_element_type=F32)


def local(
    inputs,
    block_order,
    first_gain,
    first_shift,
    second_gain,
    second_shift,
    qkv_weight,
    qkv_bias,
    out_weight,
    out_bias,
    up_weight,
    up_bias,
    down_weight,
    down_bias,
    out_grad,
):
    micro, block_rows, seqs, width = inputs.shape
    fsdp, ctx = lax.axis_size("fsdp"), lax.axis_size("ctx")
    z = lax.axis_index("ctx")
    rows = up_weight.shape[0]
    head_width, hidden_width = qkv_weight.shape[2], up_weight.shape[1]
    groups = head_width // LANES
    tokens = micro * block_rows
    order = block_order[:, 0]

    bits = [1 << i for i in range(fsdp.bit_length() - 1)]
    bit_orders = (bits, bits[::-1])

    attention_shard = jnp.concatenate([qkv_weight, jnp.transpose(out_weight)[None]], axis=0)
    attention_shard = jnp.transpose(attention_shard.reshape(4, rows, groups, LANES), (1, 2, 0, 3))
    attention_weight = gather_rows(attention_shard.reshape(rows, 4 * head_width), bit_orders)
    up_full = gather_rows(up_weight, bit_orders)
    down_full = gather_rows(jnp.transpose(down_weight), bit_orders)

    halves = ROT // 2
    frequency = jnp.exp(jnp.arange(halves, dtype=F32) * (-2.0 * math.log(10000.0) / ROT))
    angles = jnp.arange(ctx * block_rows, dtype=F32)[:, None] * frequency
    rest = ((0, 0), (0, HD - ROT))
    cosine = jnp.pad(jnp.tile(jnp.cos(angles), (1, 2)), rest, constant_values=1.0)
    sine = jnp.pad(jnp.tile(jnp.sin(angles), (1, 2)), rest)
    table = jnp.tile(jnp.stack([cosine, sine]), (1, 1, LANES // HD))

    values = inputs.reshape(tokens, width).astype(F32)
    grad_rows = out_grad.reshape(tokens, width)
    gains = [item.astype(F32) for item in (first_gain, first_shift, second_gain, second_shift)]
    centre = jnp.mean(values, axis=-1, keepdims=True)
    offset = values - centre
    spread = lax.rsqrt(jnp.mean(offset * offset, axis=-1, keepdims=True) + 1e-05)
    normal = offset * spread
    normed_one = (normal * gains[0] + gains[1]).astype(BF16)
    normed_two = (normal * gains[2] + gains[3]).astype(BF16)

    own_order = lax.dynamic_slice(order, (0, z), (micro, 1))[:, 0]
    bias = jnp.transpose(qkv_bias.astype(F32).reshape(3, groups, LANES), (1, 0, 2))
    packed = project(
        own_order, normed_one, grad_rows, attention_weight, bias.reshape(groups, 1, 3 * LANES), table, block_rows
    )
    attention = exchange_attention if groups == ctx else gathered_attention
    returned = jnp.stack(attention(packed, order, table), axis=1)

    up_pre = jnp.dot(normed_two, up_full, preferred_element_type=F32) + up_bias.astype(F32)
    hidden, pull = jax.vjp(lambda item: jax.nn.gelu(item, approximate=False), up_pre)
    hidden = hidden.astype(BF16)
    hidden_grad = jnp.dot(grad_rows, down_full, preferred_element_type=F32)
    up_grad = pull(hidden_grad)[0].astype(BF16)

    part = hidden_width // 2
    down_sums = jnp.concatenate(
        [
            scatter_rows(across(grad_rows, hidden[:, i * part : (i + 1) * part]), bit_orders[i])
            for i in range(2)
        ],
        axis=1,
    )
    up_sums = jnp.concatenate(
        [
            scatter_rows(across(normed_two, up_grad[:, i * part : (i + 1) * part]), bit_orders[i])
            for i in range(2)
        ],
        axis=1,
    )
    branch = against(hidden, down_full)
    normed_grad_two = against(up_grad, up_full)

    returned = returned.reshape(groups, tokens, 4 * LANES)
    flat = jnp.transpose(returned, (1, 0, 2))
    attended = flat[:, :, :LANES].reshape(tokens, head_width)
    pre_grad = flat[:, :, LANES:].reshape(tokens, 3 * head_width)
    weight_groups = attention_weight.reshape(width, groups, 4 * LANES)
    out_full = weight_groups[:, :, 3 * LANES :].reshape(width, head_width)
    qkv_full = weight_groups[:, :, : 3 * LANES].reshape(width, 3 * head_width)
    branch = branch + against(attended, out_full)
    normed_grad_one = against(pre_grad, qkv_full)

    qkv_part = across(normed_one, pre_grad).reshape(width, groups, 3 * LANES)
    out_part = across(grad_rows, attended).reshape(width, groups, LANES)
    attention_part = jnp.concatenate([qkv_part, out_part], axis=2).reshape(width, 4 * head_width)
    part = 2 * head_width
    attention_sums = jnp.concatenate(
        [scatter_rows(attention_part[:, i * part : (i + 1) * part], bit_orders[i]) for i in range(2)], axis=1
    )
    attention_sums = attention_sums.reshape(rows, groups, 4, LANES)
    qkv_sums = jnp.transpose(attention_sums[:, :, :3], (2, 0, 1, 3)).reshape(3, rows, head_width)
    out_sums = jnp.transpose(attention_sums[:, :, 3].reshape(rows, head_width))

    end_shift = out_bias.astype(F32) + down_bias.astype(F32)
    branch_low = branch.astype(BF16)
    branch_total = branch_low.astype(F32) + other_core(branch_low).astype(F32)
    outputs = (values + branch_total + end_shift).astype(BF16)

    slope = (normed_grad_one * gains[0] + normed_grad_two * gains[2]).astype(BF16)
    slope = slope.astype(F32) + other_core(slope).astype(F32)
    slope_mean = jnp.mean(slope, axis=-1, keepdims=True)
    slope_dot = jnp.mean(slope * normal, axis=-1, keepdims=True)
    input_grad = grad_rows.astype(F32) + spread * (slope - slope_mean - normal * slope_dot)

    norm_sums = jnp.stack(
        [
            jnp.sum(normed_grad_one * normal, axis=0),
            jnp.sum(normed_grad_one, axis=0),
            jnp.sum(normed_grad_two * normal, axis=0),
            jnp.sum(normed_grad_two, axis=0),
        ]
    )
    norm_sums = norm_sums + other_core(norm_sums)
    pre_sums = jnp.sum(pre_grad.astype(F32), axis=0).reshape(groups, 3, LANES)
    pre_sums = jnp.transpose(pre_sums, (1, 0, 2)).reshape(-1)
    small = jnp.concatenate(
        [
            norm_sums.reshape(-1),
            jnp.sum(grad_rows.astype(F32), axis=0),
            pre_sums,
            jnp.sum(up_grad.astype(F32), axis=0),
        ]
    )
    small = sum_small(small.reshape(-1, LANES)).reshape(-1)
    edges = [0]
    for extent in (width, width, width, width, width, 3 * head_width, hidden_width):
        edges.append(edges[-1] + extent)
    small = [small[a:b] for a, b in zip(edges[:-1], edges[1:])]
    return (
        outputs.reshape(inputs.shape),
        input_grad.astype(BF16).reshape(inputs.shape),
        small[0],
        small[1],
        small[2],
        small[3],
        qkv_sums,
        small[5].reshape(3, head_width),
        out_sums,
        small[4],
        up_sums,
        small[6],
        jnp.transpose(down_sums),
        small[4],
    )


def solution(mesh):
    placed = (
        P(None, "ctx", "fsdp", None),
        P(None, "fsdp", None),
        P(),
        P(),
        P(),
        P(),
        P(None, ("fsdp", "ctx"), "tp"),
        P(None, "tp"),
        P("tp", ("fsdp", "ctx")),
        P(),
        P(("fsdp", "ctx"), "tp"),
        P("tp"),
        P("tp", ("fsdp", "ctx")),
        P(),
        P(None, "ctx", "fsdp", None),
    )
    return jax.shard_map(
        local,
        mesh=mesh,
        in_specs=placed,
        out_specs=(
            P(None, "ctx", "fsdp", None),
            P(None, "ctx", "fsdp", None),
            P(),
            P(),
            P(),
            P(),
            P(None, ("fsdp", "ctx"), "tp"),
            P(None, "tp"),
            P("tp", ("fsdp", "ctx")),
            P(),
            P(("fsdp", "ctx"), "tp"),
            P("tp"),
            P("tp", ("fsdp", "ctx")),
            P(),
        ),
        check_vma=False,
    )
```

time: 1410 us -> 585 us (0.41)
  waiting for transfers between devices: 847 us -> 171 us
  matrix products: 238 us -> 68.2 us
  starting transfers between devices: 1.07 us -> 140 us
  blocking collectives: 79.5 us -> 0 us
  local copies, waits for them, and re-layouts: 137 us -> 101 us
  between operations: 19.2 us -> 2.59 us
  Pallas kernels: 0 us -> 15.1 us
    reduce_scatter x9 -> x0, waiting for transfers between devices: 550 us -> none  [the longest x1 183 us: local(): lax.psum_scatter(grad_down, ('fsdp', 'ctx'), scatter_dimension=1, tiled=T...]
    ppermute x0 -> x88, waiting for transfers between devices: none -> 171 us  [the longest x45 110 us: rotate_ring(): lax.ppermute(value, axis, [(i, (i + step) % size) for i in range(size)])]
    dot_general x102 -> x12, matrix products: 238 us -> 68.2 us  [the longest x6 21.9 us: across(): lax.dot_general(lhs, rhs, (((0,), (0,)), ((), ())), preferred_element_typ...]
    unnamed x22 -> x0, waiting for transfers between devices: 149 us -> none
    all_gather x10 -> x0, waiting for transfers between devices: 148 us -> none  [the longest x1 63.9 us: local(): lax.all_gather(qkv_weight, ('fsdp', 'ctx'), axis=1, tiled=True)]
    ppermute x0 -> x88, starting transfers between devices: none -> 140 us  [the longest x45 91.1 us: rotate_ring(): lax.ppermute(value, axis, [(i, (i + step) % size) for i in range(size)])]
    psum x1 -> x0, blocking collectives: 79.5 us -> none  [local(): lax.psum((small_list[0], small_list[1], small_list[2], small_list[3], sma...]
    dynamic_update_slice x0 -> x41, local copies, waits for them, and re-layouts: none -> 33.5 us  [place(): return lax.dynamic_update_slice(buffer, value, starts)]
  transfers between devices with their start and end apart: 21 -> 88, of which waited for: 15 -> 34; matrix products, arithmetic and copies ran while one was open for 31% -> 41% of each run, Pallas kernels for 0% -> 0%
where the time goes in v1:
time: 585 us; the launch traced here: 578 us
  waiting for transfers between devices  171 us (29%)
  starting transfers between devices  140 us (24%)
  local copies, waits for them, and re-layouts  101 us (17%)
  other arithmetic  80.3 us (14%)
  matrix products  68.2 us (12%)
  Pallas kernels  15.1 us (3%)
    ppermute x45, waiting for transfers between devices, rotate_ring(): lax.ppermute(value, axis, [(i, (i + step) % size) for i in range(size)])  110 us
    ppermute x45, starting transfers between devices, rotate_ring(): lax.ppermute(value, axis, [(i, (i + step) % size) for i in range(size)])  91.1 us
    ppermute x40, waiting for transfers between devices, swap_bit(): return lax.ppermute(value, axis, [(i, i ^ bit) for i in range(size)])  60.4 us
    ppermute x40, starting transfers between devices, swap_bit(): return lax.ppermute(value, axis, [(i, i ^ bit) for i in range(size)])  48.7 us
    dynamic_update_slice x41, local copies, waits for them, and re-layouts, place(): return lax.dynamic_update_slice(buffer, value, starts)  33.5 us
    pallas_call x3, other arithmetic, attend(): pl.pallas_call(lambda *refs: attend_kernel(blocks, block_rows, HD ** (-0....  27.3 us
    dot_general x6, matrix products, across(): lax.dot_general(lhs, rhs, (((0,), (0,)), ((), ())), preferred_element_typ...  21.9 us
    dot_general x1, matrix products, local(): jnp.dot(normed_two, up_full, preferred_element_type=F32)  19.5 us
  transfers between devices with their start and end apart: 88, of which 34 were waited for; matrix products, arithmetic and copies ran while one was open for 41% of the time, Pallas kernels for 0%

profile of v1, /device:TPU:0, one launch (start us, length us, event | category | flops | bytes accessed | tf_op | source)
XLA Modules:
  0.0 577.9 jit_solution(8154406460498615946)
XLA Ops:
  33.4 6.5 %collective-permute-start.9 = (bf16[64,2048]{1,0:T(8,128)(2,1)S(1)}, bf16[64,2048]{1,0:T(8,128)(2,1)S(1)}, u32[]{:S(2)}, u32[]{:S(2)}) collective-permute-start(bf16[64,2048]{1,0:T(8,128)(2,1)S(1)} %bitcast.275), channel_id=1, source_target_pairs={{0,2},{2,4},{4,6},{6,0},{1,3},{3,5},{5,7},{7,1},{8,10},{10,12},{12... | collective-permute-start | bytes 786440 | tf_op jit(solution)/shard_map/ppermute | solution.py:20
  49.5 8.0 %collective-permute-done.19 = bf16[64,2048]{1,0:T(8,128)(2,1)} collective-permute-done((bf16[64,2048]{1,0:T(8,128)(2,1)S(1)}, bf16[64,2048]{1,0:T(8,128)(2,1)}, u32[]{:S(2)}, u32[]{:S(2)}) %collective-permute-start.19) | collective-permute-done | bytes 262176 | tf_op jit(solution)/shard_map/ppermute | solution.py:20
  109.1 8.9 %collective-permute-done.6 = bf16[256,1024]{1,0:T(8,128)(2,1)S(1)} collective-permute-done((bf16[256,1024]{1,0:T(8,128)(2,1)}, bf16[256,1024]{1,0:T(8,128)(2,1)S(1)}, u32[]{:S(2)}, u32[]{:S(2)}) %collective-permute-start.6) | collective-permute-done | bytes 524320 | tf_op jit(solution)/shard_map/ppermute | solution.py:25
  118.6 10.7 %collective-permute-done.5 = bf16[256,1024]{1,0:T(8,128)(2,1)S(1)} collective-permute-done((bf16[256,1024]{1,0:T(8,128)(2,1)}, bf16[256,1024]{1,0:T(8,128)(2,1)S(1)}, u32[]{:S(2)}, u32[]{:S(2)}) %collective-permute-start.5) | collective-permute-done | bytes 524320 | tf_op jit(solution)/shard_map/ppermute | solution.py:25
  134.8 9.4 %collective-permute-done.8 = bf16[256,1024]{1,0:T(8,128)(2,1)S(1)} collective-permute-done((bf16[256,1024]{1,0:T(8,128)(2,1)S(1)}, bf16[256,1024]{1,0:T(8,128)(2,1)S(1)}, u32[]{:S(2)}, u32[]{:S(2)}) %collective-permute-start.8) | collective-permute-done | bytes 524320 | tf_op jit(solution)/shard_map/ppermute | solution.py:25
  145.6 19.5 %multiply_convert_fusion = (bf16[768,2048]{1,0:T(8,128)(2,1)}, f32[768,2048]{1,0:T(8,128)S(1)}, f32[768,2048]{1,0:T(8,128)}) fusion(f32[2048]{0:T(1024)S(1)} %convert_element_type.323, bf16[768,1024]{1,0:T(8,128)(2,1)S(1)} %copy-done.23, bf16[1024,2048]{1,0:T(8,128)(2,1)} %constant_dynamic-update-slice_fusion.32), kind=kOutput, calls=%fused_computation.13 | convolution fusion | flops 3325034496 | bytes 21504000 | tf_op jit(solution)/shard_map/dot_general | solution.py:378
  169.9 6.0 %collective-permute-done.17 = bf16[256,1024]{1,0:T(8,128)(2,1)S(1)} collective-permute-done((bf16[256,1024]{1,0:T(8,128)(2,1)S(1)}, bf16[256,1024]{1,0:T(8,128)(2,1)S(1)}, u32[]{:S(2)}, u32[]{:S(2)}) %collective-permute-start.17) | collective-permute-done | bytes 524320 | tf_op jit(solution)/shard_map/ppermute | solution.py:25
  176.0 9.3 %convert_reduce_fusion = (f32[2048]{0:T(1024)S(1)}, bf16[768,2048]{1,0:T(8,128)(2,1)S(1)}) fusion(f32[768,2048]{1,0:T(8,128)S(1)} %get-tuple-element.101, bf16[768,1024]{1,0:T(8,128)(2,1)S(1)} %bitcast.262, bf16[1024,2048]{1,0:T(8,128)(2,1)S(1)} %constant_dynamic-update-slice_fusion.28, f32[768,2048]{1,0:T(8,128)} %get-tuple-element.178, ...), kind=kOutput, calls=%fused_computation.12 | convolution fusion | flops 3247962112 | bytes 21512192 | tf_op jit(solution)/shard_map/dot_general | solution.py:381
  203.5 15.1 %shard_map.254 = bf16[4,3,256,512]{3,2,1,0:T(8,128)(2,1)} custom-call(s32[3]{0:T(128)} %fusion.66.order_ref, bf16[768,1024]{1,0:T(8,128)(2,1)} %get-tuple-element.129.normed_ref, bf16[768,1024]{1,0:T(8,128)(2,1)} %bitcast.260, bf16[1024,2048]{1,0:T(8,128)(2,1)} %constant_dynamic-update-slice_fusion.24.weight_ref, f32[4,1,384]{2,1,0:T(1,128)} %copy.40.bias_ref, ...), custom_call_target="tpu_custom_call" | custom-call | flops 3221225472 | bytes 10485760 | tf_op jit(solution)/shard_map/pallas_call | solution.py:110
  221.7 6.2 %collective-permute-start.39 = (bf16[256,512]{1,0:T(8,128)(2,1)S(1)}, bf16[256,512]{1,0:T(8,128)(2,1)S(1)}, u32[]{:S(2)}, u32[]{:S(2)}) collective-permute-start(bf16[256,512]{1,0:T(8,128)(2,1)S(1)} %get-tuple-element.119), channel_id=1, source_target_pairs={{0,2},{2,4},{4,6},{6,0},{1,3},{3,5},{5,7},{7,1},{8,10},{10,12},{12... | collective-permute-start | bytes 786440 | tf_op jit(solution)/shard_map/ppermute | solution.py:20
  245.7 13.9 %collective-permute-done.40 = bf16[256,512]{1,0:T(8,128)(2,1)S(1)} collective-permute-done((bf16[256,512]{1,0:T(8,128)(2,1)S(1)}, bf16[256,512]{1,0:T(8,128)(2,1)S(1)}, u32[]{:S(2)}, u32[]{:S(2)}) %collective-permute-start.40) | collective-permute-done | bytes 262176 | tf_op jit(solution)/shard_map/ppermute | solution.py:20
  264.9 9.6 %shard_map.255 = (bf16[4,1,256,512]{3,2,1,0:T(8,128)(2,1)S(1)}, bf16[256,512]{1,0:T(8,128)(2,1)}, bf16[256,512]{1,0:T(8,128)(2,1)}, bf16[256,512]{1,0:T(8,128)(2,1)}) fusion(bf16[4,1,256,512]{3,2,1,0:T(8,128)(2,1)S(1)} %stack.65.clone, s32[]{:T(128)S(6)} %select_n.314, s32[4]{0:T(128)S(1)} %pad_add_fusion.2, f32[2,1024,128]{2,1,0:T(8,128)S(1)} %copy-done.24, ...), kind=kCustom, calls=%fused_computation.130 | custom fusion | flops 2348810240 | bytes 3146244 | tf_op jit(solution)/shard_map/pallas_call | solution.py:185
  277.9 11.0 %collective-permute-start.42 = (bf16[256,512]{1,0:T(8,128)(2,1)}, bf16[256,512]{1,0:T(8,128)(2,1)}, u32[]{:S(2)}, u32[]{:S(2)}) collective-permute-start(bf16[256,512]{1,0:T(8,128)(2,1)} %get-tuple-element.85), channel_id=1, source_target_pairs={{0,6},{2,0},{4,2},{6,4},{1,7},{3,1},{5,3},{7,5},{8,14},{10,8},{12,... | collective-permute-start | bytes 786440 | tf_op jit(solution)/shard_map/ppermute | solution.py:20
  292.8 8.0 %reshape.352 = bf16[1024,4,512]{2,1,0:T(4,128)(2,1)} reshape(bf16[1024,2048]{1,0:T(8,128)(2,1)} %constant_dynamic-update-slice_fusion.24.weight_ref) | data formatting | bytes 8388608 | tf_op jit(solution)/shard_map/reshape | solution.py:406
  305.5 8.7 %shard_map.256 = (bf16[4,1,256,512]{3,2,1,0:T(8,128)(2,1)S(1)}, bf16[256,512]{1,0:T(8,128)(2,1)S(1)}, bf16[256,512]{1,0:T(8,128)(2,1)S(1)}, bf16[256,512]{1,0:T(8,128)(2,1)S(1)}) fusion(bf16[4,1,256,512]{3,2,1,0:T(8,128)(2,1)S(1)} %stack.65.clone.1, s32[]{:T(128)S(6)} %select_n.314, s32[4]{0:T(128)S(1)} %pad_add_fusion.1, ...), kind=kCustom, calls=%fused_computation.134 | custom fusion | flops 2348810240 | bytes 3146244 | tf_op jit(solution)/shard_map/pallas_call | solution.py:185
  318.1 9.0 %shard_map.257 = (bf16[4,1,256,512]{3,2,1,0:T(8,128)(2,1)S(1)}, bf16[256,512]{1,0:T(8,128)(2,1)S(1)}, bf16[256,512]{1,0:T(8,128)(2,1)S(1)}, bf16[256,512]{1,0:T(8,128)(2,1)S(1)}) fusion(bf16[4,1,256,512]{3,2,1,0:T(8,128)(2,1)S(1)} %stack.65.clone.2, s32[]{:T(128)S(6)} %select_n.314, s32[4]{0:T(128)S(1)} %pad_add_fusion, ...), kind=kCustom, calls=%fused_computation.138 | custom fusion | flops 2348810240 | bytes 3146244 | tf_op jit(solution)/shard_map/pallas_call | solution.py:185
  338.2 8.6 %collective-permute-start.37 = (bf16[256,512]{1,0:T(8,128)(2,1)S(1)}, bf16[256,512]{1,0:T(8,128)(2,1)S(1)}, u32[]{:S(2)}, u32[]{:S(2)}) collective-permute-start(bf16[256,512]{1,0:T(8,128)(2,1)S(1)} %get-tuple-element.71), channel_id=1, source_target_pairs={{0,4},{2,6},{4,0},{6,2},{1,5},{3,7},{5,1},{7,3},{8,12},{10,14},{12... | collective-permute-start | bytes 786440 | tf_op jit(solution)/shard_map/ppermute | solution.py:20
  347.0 9.8 %collective-permute-done.37 = bf16[256,512]{1,0:T(8,128)(2,1)S(1)} collective-permute-done((bf16[256,512]{1,0:T(8,128)(2,1)S(1)}, bf16[256,512]{1,0:T(8,128)(2,1)S(1)}, u32[]{:S(2)}, u32[]{:S(2)}) %collective-permute-start.37) | collective-permute-done | bytes 262176 | tf_op jit(solution)/shard_map/ppermute | solution.py:20
  357.4 7.2 %collective-permute-done.30 = bf16[256,512]{1,0:T(8,128)(2,1)S(1)} collective-permute-done((bf16[256,512]{1,0:T(8,128)(2,1)S(1)}, bf16[256,512]{1,0:T(8,128)(2,1)S(1)}, u32[]{:S(2)}, u32[]{:S(2)}) %collective-permute-start.30) | collective-permute-done | bytes 262176 | tf_op jit(solution)/shard_map/ppermute | solution.py:20
  395.1 6.8 %fusion.16 = (bf16[768,1024]{1,0:T(8,128)(2,1)}, f32[768,1024,1]{1,0,2:T(8,128)}) fusion(f32[768,1024]{1,0:T(8,128)} %fusion.90, f32[1024]{0:T(1024)S(1)} %convert_element_type.325, f32[1024]{0:T(1024)S(1)} %convert_element_type.320, bf16[1024,4,384]{2,1,0:T(4,128)(2,1)} %slice.134, bf16[768,4,512]{2,0,1:T(8,128)(2,1)S(1)} %bitcast.258), kind=kOutput, calls=%fused_computation.35 | convolution fusion | flops 2419064832 | bytes 13377536 | tf_op jit(solution)/shard_map/dot_general | solution.py:314
  471.2 6.8 %collective-permute-done.68 = bf16[64,1024]{1,0:T(8,128)(2,1)S(1)} collective-permute-done((bf16[64,1024]{1,0:T(8,128)(2,1)S(1)}, bf16[64,1024]{1,0:T(8,128)(2,1)S(1)}, u32[]{:S(2)}, u32[]{:S(2)}) %collective-permute-start.68) | collective-permute-done | bytes 131104 | tf_op jit(solution)/shard_map/ppermute | solution.py:20
  514.4 20.9 %collective-permute-done.62 = bf16[64,1024]{0,1:T(8,128)(2,1)S(1)} collective-permute-done((bf16[64,1024]{0,1:T(8,128)(2,1)S(1)}, bf16[64,1024]{0,1:T(8,128)(2,1)S(1)}, u32[]{:S(2)}, u32[]{:S(2)}) %collective-permute-start.62) | collective-permute-done | bytes 131104 | tf_op jit(solution)/shard_map/ppermute | solution.py:20
  539.7 9.3 %collective-permute-done.56 = bf16[64,1024]{0,1:T(8,128)(2,1)S(1)} collective-permute-done((bf16[64,1024]{0,1:T(8,128)(2,1)S(1)}, bf16[64,1024]{0,1:T(8,128)(2,1)S(1)}, u32[]{:S(2)}, u32[]{:S(2)}) %collective-permute-start.56) | collective-permute-done | bytes 131104 | tf_op jit(solution)/shard_map/ppermute | solution.py:20
  569.1 6.0 %fusion.39 = (bf16[768,1024]{1,0:T(8,128)(2,1)}, bf16[768,1024]{1,0:T(8,128)(2,1)}) fusion(bf16[3,256,1,1024]{3,1,2,0:T(8,128)(2,1)S(1)} %copy-done.1, bf16[768,1024]{1,0:T(8,128)(2,1)} %copy-done.10, bf16[768,1024]{1,0:T(8,128)(2,1)} %get-tuple-element.179, f32[768]{0:T(1024)S(1)} %broadcast_multiply_fusion, f32[768]{0:T(1024)S(1)} %broadcast_multiply_fusion.1, ...), kind=kLoop, calls=%fused_computation.63 | loop fusion | flops 14942208 | bytes 12599296 | tf_op jit(solution)/shard_map/convert_element_type | solution.py:460
  (439 shorter events, 340.0 us)
Async XLA Ops:
  10.2 37.2 %collective-permute-start.18 = (bf16[64,2048]{1,0:T(8,128)(2,1)S(1)}, bf16[64,2048]{1,0:T(8,128)(2,1)}, u32[]{:S(2)}, u32[]{:S(2)}) collective-permute-start(bf16[64,2048]{1,0:T(8,128)(2,1)S(1)} %reshape.335), channel_id=1, source_target_pairs={{0,2},{2,4},{4,6},{6,0},{1,3},{3,5},{5,7},{7,1},{8,10},{10,12},{12... | collective-permute-start | bytes 786440 | tf_op jit(solution)/shard_map/ppermute | solution.py:20
  11.0 46.5 %collective-permute-start.19 = (bf16[64,2048]{1,0:T(8,128)(2,1)S(1)}, bf16[64,2048]{1,0:T(8,128)(2,1)}, u32[]{:S(2)}, u32[]{:S(2)}) collective-permute-start(bf16[64,2048]{1,0:T(8,128)(2,1)S(1)} %reshape.335), channel_id=1, source_target_pairs={{0,4},{2,6},{4,0},{6,2},{1,5},{3,7},{5,1},{7,3},{8,12},{10,14},{12... | collective-permute-start | bytes 786440 | tf_op jit(solution)/shard_map/ppermute | solution.py:20
  29.5 39.8 %collective-permute-start.20 = (bf16[64,2048]{1,0:T(8,128)(2,1)S(1)}, bf16[64,2048]{1,0:T(8,128)(2,1)S(1)}, u32[]{:S(2)}, u32[]{:S(2)}) collective-permute-start(bf16[64,2048]{1,0:T(8,128)(2,1)S(1)} %reshape.335), channel_id=1, source_target_pairs={{0,6},{2,0},{4,2},{6,4},{1,7},{3,1},{5,3},{7,5},{8,14},{10,8},{12,... | collective-permute-start | bytes 786440 | tf_op jit(solution)/shard_map/ppermute | solution.py:20
  103.4 61.6 %collective-permute-start.15 = (bf16[256,1024]{1,0:T(8,128)(2,1)}, bf16[256,1024]{1,0:T(8,128)(2,1)S(1)}, u32[]{:S(2)}, u32[]{:S(2)}) collective-permute-start(bf16[256,1024]{1,0:T(8,128)(2,1)} %get-tuple-element.150), channel_id=1, source_target_pairs={{0,16},{8,24},{16,0},{24,8},{1,17},{9,25},{17,1},{25,9},{2,18},{10... | collective-permute-start | bytes 1572872 | tf_op jit(solution)/shard_map/ppermute | solution.py:25
  106.8 63.0 %collective-permute-start.16 = (bf16[256,1024]{1,0:T(8,128)(2,1)}, bf16[256,1024]{1,0:T(8,128)(2,1)S(1)}, u32[]{:S(2)}, u32[]{:S(2)}) collective-permute-start(bf16[256,1024]{1,0:T(8,128)(2,1)} %get-tuple-element.150), channel_id=1, source_target_pairs={{0,8},{8,0},{16,24},{24,16},{1,9},{9,1},{17,25},{25,17},{2,10},{10... | collective-permute-start | bytes 1572872 | tf_op jit(solution)/shard_map/ppermute | solution.py:25
  118.1 48.5 %collective-permute-start.24 = (bf16[256,1024]{1,0:T(8,128)(2,1)}, bf16[256,1024]{1,0:T(8,128)(2,1)S(1)}, u32[]{:S(2)}, u32[]{:S(2)}) collective-permute-start(bf16[256,1024]{1,0:T(8,128)(2,1)} %get-tuple-element.156), channel_id=1, source_target_pairs={{0,16},{8,24},{16,0},{24,8},{1,17},{9,25},{17,1},{25,9},{2,18},{10... | collective-permute-start | bytes 1572872 | tf_op jit(solution)/shard_map/ppermute | solution.py:25
  133.4 64.6 %collective-permute-start.25 = (bf16[256,1024]{1,0:T(8,128)(2,1)S(1)}, bf16[256,1024]{1,0:T(8,128)(2,1)S(1)}, u32[]{:S(2)}, u32[]{:S(2)}) collective-permute-start(bf16[256,1024]{1,0:T(8,128)(2,1)S(1)} %copy-done.25), channel_id=1, source_target_pairs={{0,8},{8,0},{16,24},{24,16},{1,9},{9,1},{17,25},{25,17},{2,10},{10... | collective-permute-start | bytes 1572872 | tf_op jit(solution)/shard_map/ppermute | solution.py:25
  168.1 34.6 %collective-permute-start.26 = (bf16[256,1024]{1,0:T(8,128)(2,1)S(1)}, bf16[256,1024]{1,0:T(8,128)(2,1)S(1)}, u32[]{:S(2)}, u32[]{:S(2)}) collective-permute-start(bf16[256,1024]{1,0:T(8,128)(2,1)S(1)} %collective-permute-done.24), channel_id=1, source_target_pairs={{0,8},{8,0},{16,24},{24,16},{1,9},{9,1},{17,25},{25,17},{2,10},{10... | collective-permute-start | bytes 1572872 | tf_op jit(solution)/shard_map/ppermute | solution.py:25
  236.5 37.9 %collective-permute-start.33 = (bf16[256,512]{1,0:T(8,128)(2,1)}, bf16[256,512]{1,0:T(8,128)(2,1)}, u32[]{:S(2)}, u32[]{:S(2)}) collective-permute-start(bf16[256,512]{1,0:T(8,128)(2,1)} %get-tuple-element.123), channel_id=1, source_target_pairs={{0,2},{2,4},{4,6},{6,0},{1,3},{3,5},{5,7},{7,1},{8,10},{10,12},{12... | collective-permute-start | bytes 786440 | tf_op jit(solution)/shard_map/ppermute | solution.py:20
  236.5 41.3 %collective-permute-start.34 = (bf16[256,512]{1,0:T(8,128)(2,1)S(1)}, bf16[256,512]{1,0:T(8,128)(2,1)}, u32[]{:S(2)}, u32[]{:S(2)}) collective-permute-start(bf16[256,512]{1,0:T(8,128)(2,1)S(1)} %get-tuple-element.122), channel_id=1, source_target_pairs={{0,4},{2,6},{4,0},{6,2},{1,5},{3,7},{5,1},{7,3},{8,12},{10,14},{12... | collective-permute-start | bytes 786440 | tf_op jit(solution)/shard_map/ppermute | solution.py:20
  241.4 50.2 %collective-permute-start.35 = (bf16[256,512]{1,0:T(8,128)(2,1)S(1)}, bf16[256,512]{1,0:T(8,128)(2,1)}, u32[]{:S(2)}, u32[]{:S(2)}) collective-permute-start(bf16[256,512]{1,0:T(8,128)(2,1)S(1)} %get-tuple-element.121), channel_id=1, source_target_pairs={{0,6},{2,0},{4,2},{6,4},{1,7},{3,1},{5,3},{7,5},{8,14},{10,8},{12,... | collective-permute-start | bytes 786440 | tf_op jit(solution)/shard_map/ppermute | solution.py:20
  259.6 54.6 %collective-permute-start.27 = (bf16[256,512]{1,0:T(8,128)(2,1)S(1)}, bf16[256,512]{1,0:T(8,128)(2,1)}, u32[]{:S(2)}, u32[]{:S(2)}) collective-permute-start(bf16[256,512]{1,0:T(8,128)(2,1)S(1)} %get-tuple-element.126), channel_id=1, source_target_pairs={{0,2},{2,4},{4,6},{6,0},{1,3},{3,5},{5,7},{7,1},{8,10},{10,12},{12... | collective-permute-start | bytes 786440 | tf_op jit(solution)/shard_map/ppermute | solution.py:20
  260.1 55.8 %collective-permute-start.28 = (bf16[256,512]{1,0:T(8,128)(2,1)S(1)}, bf16[256,512]{1,0:T(8,128)(2,1)}, u32[]{:S(2)}, u32[]{:S(2)}) collective-permute-start(bf16[256,512]{1,0:T(8,128)(2,1)S(1)} %get-tuple-element.125), channel_id=1, source_target_pairs={{0,4},{2,6},{4,0},{6,2},{1,5},{3,7},{5,1},{7,3},{8,12},{10,14},{12... | collective-permute-start | bytes 786440 | tf_op jit(solution)/shard_map/ppermute | solution.py:20
  274.5 41.8 %collective-permute-start.29 = (bf16[256,512]{1,0:T(8,128)(2,1)S(1)}, bf16[256,512]{1,0:T(8,128)(2,1)}, u32[]{:S(2)}, u32[]{:S(2)}) collective-permute-start(bf16[256,512]{1,0:T(8,128)(2,1)S(1)} %get-tuple-element.116), channel_id=1, source_target_pairs={{0,6},{2,0},{4,2},{6,4},{1,7},{3,1},{5,3},{7,5},{8,14},{10,8},{12,... | collective-permute-start | bytes 786440 | tf_op jit(solution)/shard_map/ppermute | solution.py:20
  277.9 49.2 %collective-permute-start.42 = (bf16[256,512]{1,0:T(8,128)(2,1)}, bf16[256,512]{1,0:T(8,128)(2,1)}, u32[]{:S(2)}, u32[]{:S(2)}) collective-permute-start(bf16[256,512]{1,0:T(8,128)(2,1)} %get-tuple-element.85), channel_id=1, source_target_pairs={{0,6},{2,0},{4,2},{6,4},{1,7},{3,1},{5,3},{7,5},{8,14},{10,8},{12,... | collective-permute-start | bytes 786440 | tf_op jit(solution)/shard_map/ppermute | solution.py:20
  291.6 37.1 %collective-permute-start.43 = (bf16[256,512]{1,0:T(8,128)(2,1)}, bf16[256,512]{1,0:T(8,128)(2,1)}, u32[]{:S(2)}, u32[]{:S(2)}) collective-permute-start(bf16[256,512]{1,0:T(8,128)(2,1)} %get-tuple-element.87), channel_id=1, source_target_pairs={{0,4},{2,6},{4,0},{6,2},{1,5},{3,7},{5,1},{7,3},{8,12},{10,14},{12... | collective-permute-start | bytes 786440 | tf_op jit(solution)/shard_map/ppermute | solution.py:20
  314.2 96.9 %collective-permute-start.71 = (bf16[256,1024]{1,0:T(8,128)(2,1)}, bf16[256,1024]{1,0:T(8,128)(2,1)}, u32[]{:S(2)}, u32[]{:S(2)}) collective-permute-start(bf16[256,1024]{1,0:T(8,128)(2,1)} %get-tuple-element.111), channel_id=1, source_target_pairs={{0,8},{8,0},{16,24},{24,16},{1,9},{9,1},{17,25},{25,17},{2,10},{10... | collective-permute-start | bytes 1572872 | tf_op jit(solution)/shard_map/ppermute | solution.py:25
  315.9 110.8 %collective-permute-start.70 = (bf16[256,1024]{1,0:T(8,128)(2,1)}, bf16[256,1024]{1,0:T(8,128)(2,1)}, u32[]{:S(2)}, u32[]{:S(2)}) collective-permute-start(bf16[256,1024]{1,0:T(8,128)(2,1)} %get-tuple-element.110), channel_id=1, source_target_pairs={{0,8},{8,0},{16,24},{24,16},{1,9},{9,1},{17,25},{25,17},{2,10},{10... | collective-permute-start | bytes 1572872 | tf_op jit(solution)/shard_map/ppermute | solution.py:25
  316.3 98.7 %collective-permute-start.65 = (bf16[256,1024]{1,0:T(8,128)(2,1)}, bf16[256,1024]{1,0:T(8,128)(2,1)}, u32[]{:S(2)}, u32[]{:S(2)}) collective-permute-start(bf16[256,1024]{1,0:T(8,128)(2,1)} %get-tuple-element.109), channel_id=1, source_target_pairs={{0,16},{8,24},{16,0},{24,8},{1,17},{9,25},{17,1},{25,9},{2,18},{10... | collective-permute-start | bytes 1572872 | tf_op jit(solution)/shard_map/ppermute | solution.py:25
  367.0 65.7 %collective-permute-start.64 = (bf16[256,1024]{1,0:T(8,128)(2,1)}, bf16[256,1024]{1,0:T(8,128)(2,1)}, u32[]{:S(2)}, u32[]{:S(2)}) collective-permute-start(bf16[256,1024]{1,0:T(8,128)(2,1)} %get-tuple-element.108), channel_id=1, source_target_pairs={{0,16},{8,24},{16,0},{24,8},{1,17},{9,25},{17,1},{25,9},{2,18},{10... | collective-permute-start | bytes 1572872 | tf_op jit(solution)/shard_map/ppermute | solution.py:25
  372.9 47.9 %collective-permute-start.83 = (bf16[256,1024]{1,0:T(8,128)(2,1)}, bf16[256,1024]{1,0:T(8,128)(2,1)}, u32[]{:S(2)}, u32[]{:S(2)}) collective-permute-start(bf16[256,1024]{1,0:T(8,128)(2,1)} %get-tuple-element.107), channel_id=1, source_target_pairs={{0,8},{8,0},{16,24},{24,16},{1,9},{9,1},{17,25},{25,17},{2,10},{10... | collective-permute-start | bytes 1572872 | tf_op jit(solution)/shard_map/ppermute | solution.py:25
  441.2 95.7 %collective-permute-start.46 = (bf16[768,1024]{1,0:T(8,128)(2,1)S(1)}, bf16[768,1024]{1,0:T(8,128)(2,1)S(1)}, u32[]{:S(2)}, u32[]{:S(2)}) collective-permute-start(bf16[768,1024]{1,0:T(8,128)(2,1)S(1)} %copy-done.9), channel_id=1, source_target_pairs={{0,1},{1,0},{2,3},{3,2},{4,5},{5,4},{6,7},{7,6},{8,9},{9,8},{10,11... | collective-permute-start | bytes 4718600 | tf_op jit(solution)/shard_map/ppermute | solution.py:84
  443.3 59.3 %collective-permute-start.58 = (bf16[256,1024]{0,1:T(8,128)(2,1)S(1)}, bf16[256,1024]{0,1:T(8,128)(2,1)S(1)}, u32[]{:S(2)}, u32[]{:S(2)}) collective-permute-start(bf16[256,1024]{0,1:T(8,128)(2,1)S(1)} %copy-done.29), channel_id=1, source_target_pairs={{0,8},{8,0},{16,24},{24,16},{1,9},{9,1},{17,25},{25,17},{2,10},{10... | collective-permute-start | bytes 1572872 | tf_op jit(solution)/shard_map/ppermute | solution.py:25
  502.7 66.4 %collective-permute-start.45 = (bf16[768,1024]{1,0:T(8,128)(2,1)}, bf16[768,1024]{1,0:T(8,128)(2,1)}, u32[]{:S(2)}, u32[]{:S(2)}) collective-permute-start(bf16[768,1024]{1,0:T(8,128)(2,1)} %fusion.18), channel_id=1, source_target_pairs={{0,1},{1,0},{2,3},{3,2},{4,5},{5,4},{6,7},{7,6},{8,9},{9,8},{10,11... | collective-permute-start | bytes 4718600 | tf_op jit(solution)/shard_map/ppermute | solution.py:84
  (122 other events, 2440.0 us)

commit v2 on v1

v2 whole, which is shorter than its diff:
```python
import math

import jax
import jax.numpy as jnp
from jax import lax
from jax.experimental import pallas as pl
from jax.experimental.pallas import tpu as pltpu
from jax.sharding import PartitionSpec as P

HD = 64
ROT = 16
LANES = 128
F32 = jnp.float32
BF16 = jnp.bfloat16
VMEM_BYTES = 56 * 1024 * 1024
EPSILON = 1e-05


def swap(value, axis, bit):
    size = lax.axis_size(axis)
    return lax.ppermute(value, axis, [(i, i ^ bit) for i in range(size)])


def sequence_of(bits):
    offsets = [0]
    for bit in bits:
        offsets += [offset | bit for offset in offsets]
    return offsets


def gather_column(shard):
    return jnp.concatenate([shard] + [swap(shard, "ctx", j) for j in range(1, lax.axis_size("ctx"))], axis=0)


def gather_pieces(column, bits):
    pieces = {0: column}
    for bit in bits:
        for offset in list(pieces):
            pieces[offset | bit] = swap(pieces[offset], "fsdp", bit)
    return [pieces[offset] for offset in range(len(pieces))]


def scatter_pieces(keep, send, bits):
    for bit in reversed(bits):
        got = swap(send, "fsdp", bit).astype(F32)
        half = keep.shape[0] // 2
        if half:
            send = (keep[half:] + got[half:]).astype(BF16)
            keep = keep[:half] + got[:half]
        else:
            keep = keep + got
    return keep[0]


def scatter_column(parts):
    ctx = lax.axis_size("ctx")
    rows = parts[0].shape[0] // ctx
    cut = lambda j: jnp.concatenate([part[j * rows : (j + 1) * rows] for part in parts], axis=1)
    total = cut(0)
    for j in range(1, ctx):
        total = total + swap(cut(j).astype(BF16), "ctx", j).astype(F32)
    return total


def sum_small(value):
    for axis in ("fsdp", "ctx"):
        bit = 1
        while bit < lax.axis_size(axis):
            value = value + swap(value, axis, bit)
            bit *= 2
    return value


def unpermute(vectors, rows):
    width = vectors.shape[-1]
    index = lax.axis_index("fsdp") * lax.axis_size("ctx") + lax.axis_index("ctx")
    blocks = vectors.reshape(-1, width // rows, rows)
    bit = 1
    while bit < width // rows:
        paired = blocks.reshape(blocks.shape[0], -1, 2, bit, rows)
        blocks = jnp.where((index & bit) != 0, paired[:, :, ::-1], paired).reshape(blocks.shape)
        bit *= 2
    return blocks.reshape(vectors.shape)


def params(**more):
    return pltpu.CompilerParams(vmem_limit_bytes=VMEM_BYTES, **more)


def matmul(lhs, rhs):
    return jnp.dot(lhs, rhs, preferred_element_type=F32)


def against(lhs, rhs):
    return lax.dot_general(lhs, rhs, (((1,), (1,)), ((), ())), preferred_element_type=F32)


def exchanged(load, width, index, rows):
    shift = index * rows
    high, low = shift // LANES, lax.rem(shift, LANES)
    blocks = []
    for block in range(width // LANES):
        start = pl.multiple_of((block ^ high) * LANES, LANES)
        value = load(pl.ds(start, LANES)).astype(F32)
        step = rows
        while step < LANES:
            lane = lax.broadcasted_iota(jnp.int32, value.shape, 1)
            turned = jnp.where((lane & step) != 0, pltpu.roll(value, step, 1), pltpu.roll(value, LANES - step, 1))
            value = jnp.where((low & step) != 0, turned, value)
            step *= 2
        blocks.append(value)
    return jnp.concatenate(blocks, axis=1)


def normal_of(values):
    centre = jnp.mean(values, axis=-1, keepdims=True)
    offset = values - centre
    spread = lax.rsqrt(jnp.mean(offset * offset, axis=-1, keepdims=True) + EPSILON)
    return offset * spread, spread


def prepare_kernel(rows, index_ref, x_ref, g_ref, gains_ref, x_out, g_out, one_out, two_out, one_t, two_t, g_t, sum_out):
    width = x_ref.shape[1]
    index = index_ref[0]
    values = exchanged(lambda lanes: x_ref[:, lanes], width, index, rows)
    grads = exchanged(lambda lanes: g_ref[:, lanes], width, index, rows)
    gains = exchanged(lambda lanes: gains_ref[:, lanes], width, index, rows)
    normal, _ = normal_of(values)
    one = normal * gains[0:1] + gains[1:2]
    two = normal * gains[2:3] + gains[3:4]
    x_out[...] = values.astype(BF16)
    g_out[...] = grads.astype(BF16)
    one_out[...] = one.astype(BF16)
    two_out[...] = two.astype(BF16)
    one_t[...] = one.T.astype(BF16)
    two_t[...] = two.T.astype(BF16)
    g_t[...] = grads.T.astype(BF16)

    @pl.when(pl.program_id(0) == 0)
    def _():
        sum_out[...] = jnp.zeros_like(sum_out)

    sum_out[...] += jnp.sum(g_ref[...].astype(F32), axis=0, keepdims=True)


def prepare(index, x, g, gains, rows, block_rows):
    tokens, width = x.shape
    row_spec = pl.BlockSpec((block_rows, width), lambda m, *_: (m, 0))
    column_spec = pl.BlockSpec((width, block_rows), lambda m, *_: (0, m))
    plain = jax.ShapeDtypeStruct((tokens, width), BF16)
    turned = jax.ShapeDtypeStruct((width, tokens), BF16)
    return pl.pallas_call(
        lambda *refs: prepare_kernel(rows, *refs),
        out_shape=[plain] * 4 + [turned] * 3 + [jax.ShapeDtypeStruct((1, width), F32)],
        grid_spec=pltpu.PrefetchScalarGridSpec(
            num_scalar_prefetch=1,
            grid=(tokens // block_rows,),
            in_specs=[row_spec, row_spec, pl.BlockSpec(gains.shape, lambda m, *_: (0, 0))],
            out_specs=[row_spec] * 4 + [column_spec] * 3 + [pl.BlockSpec((1, width), lambda m, *_: (0, 0))],
        ),
        compiler_params=params(),
        cost_estimate=pl.CostEstimate(flops=tokens * width * 30, bytes_accessed=tokens * width * 18, transcendentals=0),
        name="prepare",
    )(index, x, g, gains)


def turn(values, cosine, sine):
    lane = lax.broadcasted_iota(jnp.int32, values.shape, 1) % HD
    ahead = pltpu.roll(values, LANES - ROT // 2, 1)
    behind = pltpu.roll(values, ROT // 2, 1)
    return values * cosine + jnp.where(lane < ROT // 2, ahead, behind) * sine


def project_kernel(fsdp, groups, parts, block_rows, place_ref, order_ref, one_ref, g_ref, table_ref, bias_ref, *refs):
    qk_refs, vo_refs, out_refs = refs[:fsdp], refs[fsdp : 2 * fsdp], refs[2 * fsdp :]
    tokens, width = one_ref.shape
    span = width // fsdp
    slot = pl.program_id(0)
    qk, value, back = bias_ref[0, :, : 2 * LANES], bias_ref[0, :, 2 * LANES :], None
    for offset in range(fsdp):
        lanes = slice(offset * span, (offset + 1) * span)
        qk = qk + matmul(one_ref[:, lanes], qk_refs[offset][...])
        value = value + matmul(one_ref[:, lanes], vo_refs[offset][:, :LANES])
        part = matmul(g_ref[:, lanes], vo_refs[offset][:, LANES:])
        back = part if back is None else back + part
    pieces = []
    for m in range(tokens // block_rows):
        rows = slice(m * block_rows, (m + 1) * block_rows)
        places = pl.ds(pl.multiple_of(order_ref[m] * block_rows, block_rows), block_rows)
        cosine, sine = table_ref[0, places, :], table_ref[1, places, :]
        pieces.append(
            jnp.concatenate(
                [turn(qk[rows, :LANES], cosine, sine), turn(qk[rows, LANES:], cosine, sine), value[rows], back[rows]],
                axis=1,
            ).astype(BF16)
        )
    for index in range(groups):

        @pl.when(slot == index)
        def _():
            start = 0
            for number, count in enumerate(parts):
                for m in range(count):
                    out_refs[index * len(parts) + number][m] = pieces[start + m]
                start += count


def project(place, own_order, one, g, table, bias, qk_pieces, vo_pieces, parts, block_rows):
    tokens, width = one.shape
    fsdp = len(qk_pieces)
    groups = bias.shape[0]
    span = width // fsdp
    whole = pl.BlockSpec(one.shape, lambda s, place, order: (0, 0))
    piece = pl.BlockSpec((span, 2 * LANES), lambda s, place, order: (0, place[0] ^ s))
    shapes = [jax.ShapeDtypeStruct((count, block_rows, 4 * LANES), BF16) for count in parts] * groups
    return pl.pallas_call(
        lambda *refs: project_kernel(fsdp, groups, parts, block_rows, *refs),
        out_shape=shapes,
        grid_spec=pltpu.PrefetchScalarGridSpec(
            num_scalar_prefetch=2,
            grid=(groups,),
            in_specs=[
                whole,
                whole,
                pl.BlockSpec(table.shape, lambda s, place, order: (0, 0, 0)),
                pl.BlockSpec((1, 1, 3 * LANES), lambda s, place, order: (place[0] ^ s, 0, 0)),
            ]
            + [piece] * (2 * fsdp),
            out_specs=[pl.BlockSpec(item.shape, lambda s, place, order: (0, 0, 0)) for item in shapes],
        ),
        compiler_params=params(),
        cost_estimate=pl.CostEstimate(
            flops=2 * tokens * width * groups * 4 * LANES,
            bytes_accessed=2 * (width * groups * 4 * LANES + tokens * groups * 4 * LANES + 2 * tokens * width),
            transcendentals=0,
        ),
        name="project",
    )(place, own_order, one, g, table, bias, *qk_pieces, *vo_pieces)


def attend_kernel(blocks, block_rows, scale, rank_ref, table_ref, *refs):
    chunk_refs, out_refs = refs[:blocks], refs[blocks : 2 * blocks]
    q_s, k_s, v_s, d_s, kt_s, vt_s, ot_s, qt_s, dk_s, dv_s = refs[2 * blocks :]
    item = pl.program_id(0)

    def rows_of(index):
        return pl.ds(pl.multiple_of(rank_ref[item * blocks + index] * block_rows, block_rows), block_rows)

    for index in range(blocks):
        rows = rows_of(index)
        q_s[rows, :] = chunk_refs[index][0, :, :LANES]
        k_s[rows, :] = chunk_refs[index][0, :, LANES : 2 * LANES]
        v_s[rows, :] = chunk_refs[index][0, :, 2 * LANES : 3 * LANES]
        d_s[rows, :] = chunk_refs[index][0, :, 3 * LANES :]
    kt_s[...] = k_s[...].T
    vt_s[...] = v_s[...].T
    lane = lax.broadcasted_iota(jnp.int32, (block_rows, LANES), 1)
    for rank in reversed(range(blocks)):
        rows = slice(rank * block_rows, (rank + 1) * block_rows)
        keys = slice(0, (rank + 1) * block_rows)
        dk, dv = None, None
        for head in range(LANES // HD):
            inside = (lane // HD) == head
            heads = slice(head * HD, (head + 1) * HD)
            q_h = jnp.where(inside, q_s[rows, :], 0).astype(BF16)
            d_h = jnp.where(inside, d_s[rows, :], 0).astype(BF16)
            scores = against(k_s[keys, :], q_h) * scale
            weights = jnp.exp(scores - jnp.max(scores, axis=0, keepdims=True))
            weights = weights * (1.0 / jnp.sum(weights, axis=0, keepdims=True))
            low = weights.astype(BF16)
            ot_s[heads, rows] = matmul(vt_s[heads, keys], low)
            dv_part = matmul(low, d_h)
            slope = against(v_s[keys, :], d_h)
            delta = jnp.sum(weights * slope, axis=0, keepdims=True)
            slope = (weights * (slope - delta)).astype(BF16)
            qt_s[heads, rows] = matmul(kt_s[heads, keys], slope)
            dk_part = matmul(slope, q_h)
            dk, dv = (dk_part, dv_part) if dk is None else (dk + dk_part, dv + dv_part)
        if rank == blocks - 1:
            dk_s[...], dv_s[...] = dk, dv
        else:
            dk_s[keys, :] += dk
            dv_s[keys, :] += dv
    for index in range(blocks):
        rows = rows_of(index)
        cosine, sine = table_ref[0, rows, :], -table_ref[1, rows, :]
        out_refs[index][0, :, :LANES] = turn(qt_s[:, rows].T * scale, cosine, sine).astype(BF16)
        out_refs[index][0, :, LANES : 2 * LANES] = turn(dk_s[rows, :] * scale, cosine, sine).astype(BF16)
        out_refs[index][0, :, 2 * LANES : 3 * LANES] = dv_s[rows, :].astype(BF16)
        out_refs[index][0, :, 3 * LANES :] = ot_s[:, rows].T.astype(BF16)


def attend(ranks, table, chunks):
    blocks = len(chunks)
    count, block_rows, _ = chunks[0].shape
    length = blocks * block_rows
    spec = pl.BlockSpec((1, block_rows, 4 * LANES), lambda m, *_: (m, 0, 0))
    pairs = count * blocks * (blocks + 1) // 2 * block_rows * block_rows
    return pl.pallas_call(
        lambda *refs: attend_kernel(blocks, block_rows, HD ** (-0.5), *refs),
        out_shape=[jax.ShapeDtypeStruct(chunk.shape, BF16) for chunk in chunks],
        grid_spec=pltpu.PrefetchScalarGridSpec(
            num_scalar_prefetch=1,
            grid=(count,),
            in_specs=[pl.BlockSpec(table.shape, lambda m, *_: (0, 0, 0))] + [spec] * blocks,
            out_specs=[spec] * blocks,
            scratch_shapes=[pltpu.VMEM((length, LANES), BF16)] * 4
            + [pltpu.VMEM((LANES, length), BF16)] * 2
            + [pltpu.VMEM((LANES, length), F32)] * 2
            + [pltpu.VMEM((length, LANES), F32)] * 2,
        ),
        compiler_params=params(),
        cost_estimate=pl.CostEstimate(
            flops=pairs * 2 * 2 * LANES * 7 * 2,
            bytes_accessed=count * length * 4 * LANES * 4,
            transcendentals=pairs * 2,
        ),
        name="attend",
    )(ranks, table, *chunks)


def forward_kernel(fsdp, up_sequence, down_sequence, two_ref, g_ref, two_t, g_t, bias_ref, *refs):
    up_refs, down_refs = refs[:fsdp], refs[fsdp : 2 * fsdp]
    branch_ref, slope_ref, up_keep, up_send, down_keep, down_send, sum_ref = refs[2 * fsdp :]
    tokens, width = two_ref.shape
    span = width // fsdp
    lanes = [slice(offset * span, (offset + 1) * span) for offset in range(fsdp)]

    @pl.when(pl.program_id(0) == 0)
    def _():
        branch_ref[...] = jnp.zeros_like(branch_ref)
        slope_ref[...] = jnp.zeros_like(slope_ref)

    pre, back = bias_ref[...], None
    for offset in range(fsdp):
        pre = pre + matmul(two_ref[:, lanes[offset]], up_refs[offset][...])
        part = matmul(g_ref[:, lanes[offset]], down_refs[offset][...])
        back = part if back is None else back + part
    gate = 0.5 * (1.0 + lax.erf(pre * math.sqrt(0.5)))
    bell = jnp.exp(-0.5 * pre * pre) * (1.0 / math.sqrt(2.0 * math.pi))
    hidden = (pre * gate).astype(BF16)
    pre_grad = (back * (gate + pre * bell)).astype(BF16)
    sum_ref[...] = jnp.sum(pre_grad.astype(F32), axis=0, keepdims=True)
    for offset in range(fsdp):
        branch_ref[:, lanes[offset]] += against(hidden, down_refs[offset][...])
        slope_ref[:, lanes[offset]] += against(pre_grad, up_refs[offset][...])
    half = fsdp // 2
    for number in range(fsdp):
        up_part = matmul(two_t[lanes[up_sequence[number]], :], pre_grad)
        down_part = matmul(g_t[lanes[down_sequence[number]], :], hidden)
        if number < half:
            up_keep[number], down_keep[number] = up_part, down_part
        else:
            up_send[number - half], down_send[number - half] = up_part.astype(BF16), down_part.astype(BF16)


def feed_forward(two, g, two_t, g_t, bias, up_pieces, down_pieces, up_sequence, down_sequence):
    tokens, width = two.shape
    fsdp = len(up_pieces)
    span, hidden = up_pieces[0].shape
    tile = 256
    half = fsdp // 2
    whole = pl.BlockSpec((tokens, width), lambda n: (0, 0))
    whole_t = pl.BlockSpec((width, tokens), lambda n: (0, 0))
    piece = pl.BlockSpec((span, tile), lambda n: (0, n))
    stack = pl.BlockSpec((half, span, tile), lambda n: (0, 0, n))
    line = pl.BlockSpec((1, tile), lambda n: (0, n))
    keep = jax.ShapeDtypeStruct((half, span, hidden), F32)
    send = jax.ShapeDtypeStruct((half, span, hidden), BF16)
    return pl.pallas_call(
        lambda *refs: forward_kernel(fsdp, up_sequence, down_sequence, *refs),
        out_shape=[jax.ShapeDtypeStruct((tokens, width), F32)] * 2
        + [keep, send, keep, send, jax.ShapeDtypeStruct((1, hidden), F32)],
        grid=(hidden // tile,),
        in_specs=[whole, whole, whole_t, whole_t, line] + [piece] * (2 * fsdp),
        out_specs=[whole, whole, stack, stack, stack, stack, line],
        compiler_params=params(),
        cost_estimate=pl.CostEstimate(
            flops=2 * tokens * width * hidden * 6,
            bytes_accessed=4 * width * hidden + 12 * width * hidden + 16 * tokens * width,
            transcendentals=2 * tokens * hidden,
        ),
        name="feed_forward",
    )(two, g, two_t, g_t, bias, *up_pieces, *down_pieces)


def finish_kernel(fsdp, groups, parts, qk_sequence, vo_sequence, place_ref, x_ref, one_t, g_t, gains_ref, branch_ref, slope_ref, *refs):
    count = groups * len(parts)
    back_refs, qk_refs, vo_refs = refs[:count], refs[count : count + fsdp], refs[count + fsdp : count + 2 * fsdp]
    both_ref, qk_keep, qk_send, vo_keep, vo_send, norm_ref, bias_ref, stack_s, one_s, out_s = refs[count + 2 * fsdp :]
    tokens, width = x_ref.shape
    block_rows = back_refs[0].shape[1]
    span = width // fsdp
    half = fsdp // 2
    lanes = [slice(offset * span, (offset + 1) * span) for offset in range(fsdp)]
    for slot in range(groups):
        start = 0
        for number, extent in enumerate(parts):
            for m in range(extent):
                rows = slice((start + m) * block_rows, (start + m + 1) * block_rows)
                stack_s[slot, rows, :] = back_refs[slot * len(parts) + number][m]
            start += extent
    one_s[...] = jnp.zeros_like(one_s)
    out_s[...] = branch_ref[...]

    def slot_step(slot, carry):
        group = place_ref[0] ^ slot
        columns = pl.ds(pl.multiple_of(group * 2 * LANES, 2 * LANES), 2 * LANES)
        first = pl.ds(pl.multiple_of(group * 2 * LANES, LANES), LANES)
        second = pl.ds(pl.multiple_of(group * 2 * LANES + LANES, LANES), LANES)
        dqk = stack_s[slot, :, : 2 * LANES]
        dv = stack_s[slot, :, 2 * LANES : 3 * LANES]
        out = stack_s[slot, :, 3 * LANES :]
        for offset in range(fsdp):
            one_s[:, lanes[offset]] += against(dqk, qk_refs[offset][:, columns]) + against(dv, vo_refs[offset][:, first])
            out_s[:, lanes[offset]] += against(out, vo_refs[offset][:, second])
        for number in range(fsdp):
            qk_part = matmul(one_t[lanes[qk_sequence[number]], :], dqk)
            dv_part = matmul(one_t[lanes[vo_sequence[number]], :], dv)
            out_part = matmul(g_t[lanes[vo_sequence[number]], :], out)
            if number < half:
                qk_keep[number, :, columns] = qk_part
                vo_keep[number, :, first] = dv_part
                vo_keep[number, :, second] = out_part
            else:
                qk_send[number - half, :, columns] = qk_part.astype(BF16)
                vo_send[number - half, :, first] = dv_part.astype(BF16)
                vo_send[number - half, :, second] = out_part.astype(BF16)
        bias_ref[pl.ds(group, 1), :] = jnp.sum(stack_s[slot, :, : 3 * LANES].astype(F32), axis=0, keepdims=True)
        return carry

    lax.fori_loop(0, groups, slot_step, 0)
    normal, _ = normal_of(x_ref[...].astype(F32))
    one, two = one_s[...], slope_ref[...]
    norm_ref[0:1, :] = jnp.sum(one * normal, axis=0, keepdims=True)
    norm_ref[1:2, :] = jnp.sum(one, axis=0, keepdims=True)
    norm_ref[2:3, :] = jnp.sum(two * normal, axis=0, keepdims=True)
    norm_ref[3:4, :] = jnp.sum(two, axis=0, keepdims=True)
    both_ref[0] = out_s[...].astype(BF16)
    both_ref[1] = (one * gains_ref[0:1, :] + two * gains_ref[2:3, :]).astype(BF16)


def finish(place, x, one_t, g_t, gains, branch, slope, returned, qk_pieces, vo_pieces, qk_sequence, vo_sequence, parts):
    tokens, width = x.shape
    fsdp = len(qk_pieces)
    groups = len(returned) // len(parts)
    span, columns = qk_pieces[0].shape
    half = fsdp // 2
    spec = pl.BlockSpec(memory_space=pltpu.VMEM)
    keep = jax.ShapeDtypeStruct((half, span, columns), F32)
    send = jax.ShapeDtypeStruct((half, span, columns), BF16)
    arrays = [x, one_t, g_t, gains, branch, slope, *returned, *qk_pieces, *vo_pieces]
    return pl.pallas_call(
        lambda *refs: finish_kernel(fsdp, groups, parts, qk_sequence, vo_sequence, *refs),
        out_shape=[
            jax.ShapeDtypeStruct((2, tokens, width), BF16),
            keep,
            send,
            keep,
            send,
            jax.ShapeDtypeStruct((4, width), F32),
            jax.ShapeDtypeStruct((groups, 3 * LANES), F32),
        ],
        in_specs=[pl.BlockSpec(memory_space=pltpu.SMEM)] + [spec] * len(arrays),
        out_specs=[spec] * 7,
        scratch_shapes=[
            pltpu.VMEM((groups, tokens, 4 * LANES), BF16),
            pltpu.VMEM((tokens, width), F32),
            pltpu.VMEM((tokens, width), F32),
        ],
        compiler_params=params(),
        cost_estimate=pl.CostEstimate(
            flops=2 * tokens * width * groups * 4 * LANES * 2,
            bytes_accessed=20 * tokens * width + 8 * width * columns * 2,
            transcendentals=0,
        ),
        name="finish",
    )(place, *arrays)


def close_kernel(rows, index_ref, x_ref, g_ref, own_ref, other_ref, shift_ref, out_ref, grad_ref, out_s, grad_s):
    width = x_ref.shape[1]
    values = x_ref[...].astype(F32)
    normal, spread = normal_of(values)
    out_s[...] = values + (own_ref[0].astype(F32) + other_ref[0].astype(F32))
    slope = own_ref[1].astype(F32) + other_ref[1].astype(F32)
    slope_mean = jnp.mean(slope, axis=-1, keepdims=True)
    slope_dot = jnp.mean(slope * normal, axis=-1, keepdims=True)
    grad_s[...] = g_ref[...].astype(F32) + spread * (slope - slope_mean - normal * slope_dot)
    out_ref[...] = (exchanged(lambda lanes: out_s[:, lanes], width, index_ref[0], rows) + shift_ref[...]).astype(BF16)
    grad_ref[...] = exchanged(lambda lanes: grad_s[:, lanes], width, index_ref[0], rows).astype(BF16)


def close(index, x, g, own, other, shift, rows, block_rows):
    tokens, width = x.shape
    row_spec = pl.BlockSpec((block_rows, width), lambda m, *_: (m, 0))
    both_spec = pl.BlockSpec((2, block_rows, width), lambda m, *_: (0, m, 0))
    return pl.pallas_call(
        lambda *refs: close_kernel(rows, *refs),
        out_shape=[jax.ShapeDtypeStruct((tokens, width), BF16)] * 2,
        grid_spec=pltpu.PrefetchScalarGridSpec(
            num_scalar_prefetch=1,
            grid=(tokens // block_rows,),
            in_specs=[row_spec, row_spec, both_spec, both_spec, pl.BlockSpec((1, width), lambda m, *_: (0, 0))],
            out_specs=[row_spec] * 2,
            scratch_shapes=[pltpu.VMEM((block_rows, width), F32)] * 2,
        ),
        compiler_params=params(),
        cost_estimate=pl.CostEstimate(flops=tokens * width * 30, bytes_accessed=tokens * width * 16, transcendentals=0),
        name="close",
    )(index, x, g, own, other, shift)


def exchange_attention(packed, order, table, parts):
    groups = len(packed) // len(parts)
    z = lax.axis_index("ctx")
    sources = z ^ jnp.arange(groups, dtype=jnp.int32)
    ranks = jnp.sum(jnp.where(sources[:, None] == jnp.arange(groups)[None, :], order[:, None, :], 0), axis=-1)
    returned = [None] * len(packed)
    start = 0
    for number, count in enumerate(parts):
        chunks = [packed[slot * len(parts) + number] for slot in range(groups)]
        chunks = [chunk if slot == 0 else swap(chunk, "ctx", slot) for slot, chunk in enumerate(chunks)]
        outs = attend(ranks[start : start + count].reshape(-1), table, chunks)
        for slot in range(groups):
            returned[slot * len(parts) + number] = outs[slot] if slot == 0 else swap(outs[slot], "ctx", slot)
        start += count
    return returned


def gathered_attention(packed, order, table, parts):
    groups = len(packed) // len(parts)
    micro, block_rows = order.shape[0], packed[0].shape[1]
    z = lax.axis_index("ctx")
    heads = groups * LANES // HD
    scale = HD ** (-0.5)
    slots = [
        jnp.concatenate([packed[slot * len(parts) + number] for number in range(len(parts))], axis=0)
        for slot in range(groups)
    ]
    packed = jnp.stack(slots)

    def split(array):
        array = array.reshape(groups, block_rows, LANES // HD, HD)
        return jnp.transpose(array, (1, 0, 2, 3)).reshape(block_rows, heads, HD)

    def join(array):
        return jnp.transpose(array.reshape(block_rows, groups, LANES), (1, 0, 2))

    results = []
    for m in range(micro):
        own = jnp.sum(jnp.where(jnp.arange(order.shape[1]) == z, order[m], 0))
        parted = packed[:, m].reshape(groups, block_rows, 4, LANES)
        queries, keys, values, douts = (split(parted[:, :, i]) for i in range(4))
        all_keys = lax.all_gather(keys, "ctx", axis=0)
        all_values = lax.all_gather(values, "ctx", axis=0)
        allowed = order[m] <= own

        def peak_step(state, item):
            key, value, ok = item
            peak, total, sums = state
            scores = jnp.einsum("bhe,rhe->hbr", queries, key, preferred_element_type=F32) * scale
            scores = jnp.where(ok, scores, -1e30)
            new = jnp.maximum(peak, jnp.max(scores, axis=-1))
            weights = jnp.where(ok, jnp.exp(scores - new[..., None]), 0.0)
            fade = jnp.exp(peak - new)
            part = jnp.einsum("hbr,rhe->hbe", weights.astype(BF16), value, preferred_element_type=F32)
            return (new, total * fade + jnp.sum(weights, axis=-1), sums * fade[..., None] + part), None

        start = (
            jnp.full((heads, block_rows), -1e30, F32),
            jnp.zeros((heads, block_rows), F32),
            jnp.zeros((heads, block_rows, HD), F32),
        )
        (peak, total, sums), _ = lax.scan(peak_step, start, (all_keys, all_values, allowed))
        attended = jnp.transpose(sums / total[..., None], (1, 0, 2))
        level = peak + jnp.log(total)
        delta = jnp.transpose(jnp.sum(douts.astype(F32) * attended, axis=-1))

        def back_step(query_sum, item):
            key, value, ok = item
            scores = jnp.einsum("bhe,rhe->hbr", queries, key, preferred_element_type=F32) * scale
            weights = jnp.where(ok, jnp.exp(scores - level[..., None]), 0.0)
            value_grad = jnp.einsum("hbr,bhe->rhe", weights.astype(BF16), douts, preferred_element_type=F32)
            slope = jnp.einsum("bhe,rhe->hbr", douts, value, preferred_element_type=F32)
            slope = (weights * (slope - delta[..., None])).astype(BF16)
            query_part = jnp.einsum("hbr,rhe->bhe", slope, key, preferred_element_type=F32) * scale
            key_grad = jnp.einsum("hbr,bhe->rhe", slope, queries, preferred_element_type=F32) * scale
            return query_sum + query_part, (key_grad.astype(BF16), value_grad.astype(BF16))

        query_grad, (key_grads, value_grads) = lax.scan(
            back_step, jnp.zeros(queries.shape, F32), (all_keys, all_values, allowed)
        )
        key_grad = lax.psum_scatter(key_grads, "ctx", scatter_dimension=0).astype(F32)
        value_grad = lax.psum_scatter(value_grads, "ctx", scatter_dimension=0)
        rows = lax.dynamic_slice(table, (0, own * block_rows, 0), (2, block_rows, LANES))

        def unturn(array):
            half = ROT // 2
            cosine, sine = rows[0, :, :half][:, None], rows[1, :, half:ROT][:, None]
            first, second = array[..., :half], array[..., half:ROT]
            return jnp.concatenate(
                [first * cosine + second * sine, second * cosine - first * sine, array[..., ROT:]], axis=-1
            )

        fields = (unturn(query_grad), unturn(key_grad), value_grad, attended)
        results.append(jnp.concatenate([join(field.astype(BF16)) for field in fields], axis=-1))
    results = jnp.stack(results, axis=1)
    edges = [sum(parts[:number]) for number in range(len(parts) + 1)]
    return [results[slot, a:b] for slot in range(groups) for a, b in zip(edges[:-1], edges[1:])]


def rotation_table(length):
    lane = jnp.arange(LANES, dtype=jnp.int32) % HD
    halves = ROT // 2
    frequency = jnp.exp((lane % halves).astype(F32) * (-2.0 * math.log(10000.0) / ROT))
    frequency = jnp.where(lane < ROT, frequency, 0.0)
    angles = jnp.arange(length, dtype=F32)[:, None] * frequency
    return jnp.stack([jnp.cos(angles), jnp.where(lane < halves, -1.0, 1.0) * jnp.sin(angles)])


def local(
    inputs,
    block_order,
    first_gain,
    first_shift,
    second_gain,
    second_shift,
    qkv_weight,
    qkv_bias,
    out_weight,
    out_bias,
    up_weight,
    up_bias,
    down_weight,
    down_bias,
    out_grad,
):
    micro, block_rows, _, width = inputs.shape
    fsdp, ctx = lax.axis_size("fsdp"), lax.axis_size("ctx")
    f, z = lax.axis_index("fsdp"), lax.axis_index("ctx")
    rows = up_weight.shape[0]
    head_width, hidden_width = qkv_weight.shape[2], up_weight.shape[1]
    groups = head_width // LANES
    tokens = micro * block_rows
    order = block_order[:, 0]
    parts = (1, micro - 1)
    exchanging = groups == ctx

    bits = [1 << i for i in range(fsdp.bit_length() - 1)]
    back_bits = bits[::-1]
    forth, back = sequence_of(bits), sequence_of(back_bits)

    shard = jnp.concatenate([qkv_weight, jnp.transpose(out_weight)[None]], axis=0)
    shard = jnp.transpose(shard.reshape(2, 2, rows, groups, LANES), (2, 0, 3, 1, 4)).reshape(rows, 4 * head_width)
    column = gather_column(shard)
    forward_shard = jnp.concatenate([up_weight, jnp.transpose(down_weight)], axis=1)
    forward_shard, column = lax.optimization_barrier((forward_shard, column))
    qk_pieces = gather_pieces(column[:, : 2 * head_width], bits)
    vo_pieces = gather_pieces(column[:, 2 * head_width :], back_bits)
    forward_column = gather_column(forward_shard)
    up_pieces = gather_pieces(forward_column[:, :hidden_width], bits)
    down_pieces = gather_pieces(forward_column[:, hidden_width:], back_bits)

    index = (f * ctx + z).astype(jnp.int32).reshape(1)
    gains = jnp.stack([first_gain, first_shift, second_gain, second_shift]).astype(F32)
    x, g, one, two, one_t, two_t, g_t, grad_sum = prepare(
        index, inputs.reshape(tokens, width), out_grad.reshape(tokens, width), gains, rows, block_rows
    )

    table = rotation_table(ctx * block_rows)
    place = (z if exchanging else jnp.zeros_like(z)).astype(jnp.int32).reshape(1)
    own_order = jnp.sum(jnp.where(jnp.arange(ctx)[None, :] == z, order, 0), axis=1)
    bias = jnp.transpose(qkv_bias.astype(F32).reshape(3, groups, LANES), (1, 0, 2)).reshape(groups, 1, 3 * LANES)
    packed = project(place, own_order, one, g, table, bias, qk_pieces, vo_pieces, parts, block_rows)
    attention = exchange_attention if exchanging else gathered_attention
    returned = attention(packed, order, table, parts)

    branch, slope, up_keep, up_send, down_keep, down_send, up_sum = feed_forward(
        two, g, two_t, g_t, up_bias.astype(F32).reshape(1, -1), up_pieces, down_pieces, forth, back
    )
    forward_sums = scatter_column(
        [scatter_pieces(up_keep, up_send, bits), scatter_pieces(down_keep, down_send, back_bits)]
    )

    gains_here = unpermute(gains, rows)
    both, qk_keep, qk_send, vo_keep, vo_send, norm_sums, pre_sums = finish(
        place, x, one_t, g_t, gains_here, branch, slope, returned, qk_pieces, vo_pieces, forth, back, parts
    )
    attention_sums = scatter_column(
        [scatter_pieces(qk_keep, qk_send, bits), scatter_pieces(vo_keep, vo_send, back_bits)]
    )
    attention_sums = attention_sums.reshape(rows, 2, groups, 2, LANES)
    attention_sums = jnp.transpose(attention_sums, (1, 3, 0, 2, 4)).reshape(4, rows, head_width)

    end_shift = (out_bias.astype(F32) + down_bias.astype(F32)).reshape(1, width)
    outputs, input_grad = close(index, x, g, both, swap(both, "tp", 1), end_shift, rows, block_rows)

    norm_sums = unpermute(norm_sums + swap(norm_sums, "tp", 1), rows)
    pre_sums = jnp.transpose(pre_sums.reshape(groups, 3, LANES), (1, 0, 2))
    small = [norm_sums.reshape(-1), grad_sum.reshape(-1), pre_sums.reshape(-1), up_sum.reshape(-1)]
    small = sum_small(jnp.concatenate(small).reshape(-1, LANES)).reshape(-1)
    edges = [0]
    for extent in (width, width, width, width, width, 3 * head_width, hidden_width):
        edges.append(edges[-1] + extent)
    small = [small[a:b] for a, b in zip(edges[:-1], edges[1:])]
    return (
        outputs.reshape(inputs.shape),
        input_grad.reshape(inputs.shape),
        small[0],
        small[1],
        small[2],
        small[3],
        attention_sums[:3],
        small[5].reshape(3, head_width),
        jnp.transpose(attention_sums[3]),
        small[4],
        forward_sums[:, :hidden_width],
        small[6],
        jnp.transpose(forward_sums[:, hidden_width:]),
        small[4],
    )


def solution(mesh):
    placed = (
        P(None, "ctx", "fsdp", None),
        P(None, "fsdp", None),
        P(),
        P(),
        P(),
        P(),
        P(None, ("fsdp", "ctx"), "tp"),
        P(None, "tp"),
        P("tp", ("fsdp", "ctx")),
        P(),
        P(("fsdp", "ctx"), "tp"),
        P("tp"),
        P("tp", ("fsdp", "ctx")),
        P(),
        P(None, "ctx", "fsdp", None),
    )
    return jax.shard_map(
        local,
        mesh=mesh,
        in_specs=placed,
        out_specs=(
            P(None, "ctx", "fsdp", None),
            P(None, "ctx", "fsdp", None),
            P(),
            P(),
            P(),
            P(),
            P(None, ("fsdp", "ctx"), "tp"),
            P(None, "tp"),
            P("tp", ("fsdp", "ctx")),
            P(),
            P(("fsdp", "ctx"), "tp"),
            P("tp"),
            P("tp", ("fsdp", "ctx")),
            P(),
        ),
        check_vma=False,
    )
```

time: 585 us -> 454 us (0.78)
  the two profiles are of different devices: /device:TPU:0 before, /device:TPU:10 now
where the time goes in v2:
time: 454 us; the launch traced here: 447 us
  waiting for transfers between devices  233 us (51%)
  Pallas kernels  114 us (25%)
  starting transfers between devices  59.1 us (13%)
  other arithmetic  22.5 us (5%)
  local copies, waits for them, and re-layouts  16.6 us (4%)
    ppermute x50, waiting for transfers between devices, swap(): return lax.ppermute(value, axis, [(i, i ^ bit) for i in range(size)])  233 us
    ppermute x50, starting transfers between devices, swap(): return lax.ppermute(value, axis, [(i, i ^ bit) for i in range(size)])  59.1 us
    pallas_call x2, Pallas kernels, attend(): pl.pallas_call(lambda *refs: attend_kernel(blocks, block_rows, HD ** (-0....  33.3 us
    pallas_call x1, Pallas kernels, feed_forward(): pl.pallas_call(lambda *refs: forward_kernel(fsdp, up_sequence, down_seque...  30.6 us
    pallas_call x1, Pallas kernels, finish(): pl.pallas_call(lambda *refs: finish_kernel(fsdp, groups, parts, qk_sequen...  22.8 us
    pallas_call x1, Pallas kernels, project(): pl.pallas_call(lambda *refs: project_kernel(fsdp, groups, parts, block_ro...  12.1 us
  transfers between devices with their start and end apart: 50, of which 23 were waited for; matrix products, arithmetic and copies ran while one was open for 7% of the time, Pallas kernels for 20%

profile of v2, /device:TPU:10, one launch (start us, length us, event | category | flops | bytes accessed | tf_op | source)
XLA Modules:
  0.0 446.9 jit_solution(7938560631645687575)
XLA Ops:
  11.6 7.7 %prepare.1 = (bf16[768,1024]{1,0:T(8,128)(2,1)}, bf16[768,1024]{1,0:T(8,128)(2,1)}, bf16[768,1024]{1,0:T(8,128)(2,1)}, bf16[768,1024]{1,0:T(8,128)(2,1)}, bf16[1...) custom-call(s32[1]{0:T(128)} %bitcast.refs_0_, ...), custom_call_target="tpu_custom_call" | custom-call | flops 23592960 | bytes 14155776 | tf_op jit(solution)/shard_map/prepare/pallas_call | solution.py:152
  23.5 5.1 %collective-permute-done.2 = bf16[64,2048]{1,0:T(8,128)(2,1)S(1)} collective-permute-done((bf16[64,2048]{1,0:T(8,128)(2,1)S(1)}, bf16[64,2048]{1,0:T(8,128)(2,1)S(1)}, u32[]{:S(2)}, u32[]{:S(2)}) %collective-permute-start.2) | collective-permute-done | bytes 262176 | tf_op jit(solution)/shard_map/ppermute | solution.py:21
  34.6 14.4 %collective-permute-done.3 = bf16[64,4096]{1,0:T(8,128)(2,1)S(1)} collective-permute-done((bf16[64,4096]{1,0:T(8,128)(2,1)S(1)}, bf16[64,4096]{1,0:T(8,128)(2,1)S(1)}, u32[]{:S(2)}, u32[]{:S(2)}) %collective-permute-start.3) | collective-permute-done | bytes 524320 | tf_op jit(solution)/shard_map/ppermute | solution.py:21
  50.6 16.1 %collective-permute-done.4 = bf16[64,4096]{1,0:T(8,128)(2,1)S(1)} collective-permute-done((bf16[64,4096]{1,0:T(8,128)(2,1)S(1)}, bf16[64,4096]{1,0:T(8,128)(2,1)S(1)}, u32[]{:S(2)}, u32[]{:S(2)}) %collective-permute-start.4) | collective-permute-done | bytes 524320 | tf_op jit(solution)/shard_map/ppermute | solution.py:21
  70.3 6.0 %collective-permute-done.5 = bf16[64,4096]{1,0:T(8,128)(2,1)S(1)} collective-permute-done((bf16[64,4096]{1,0:T(8,128)(2,1)S(1)}, bf16[64,4096]{1,0:T(8,128)(2,1)S(1)}, u32[]{:S(2)}, u32[]{:S(2)}) %collective-permute-start.5) | collective-permute-done | bytes 524320 | tf_op jit(solution)/shard_map/ppermute | solution.py:21
  78.6 6.3 %collective-permute-done.17.refs_13_.refs_22_ = bf16[256,1024]{1,0:T(8,128)(2,1)S(1)} collective-permute-done((bf16[256,1024]{1,0:T(8,128)(2,1)S(1)}, bf16[256,1024]{1,0:T(8,128)(2,1)S(1)}, u32[]{:S(2)}, u32[]{:S(2)}) %collective-permute-start.17) | collective-permute-done | bytes 524320 | tf_op jit(solution)/shard_map/ppermute | solution.py:21
  85.7 12.1 %project.1 = (bf16[1,256,512]{2,1,0:T(8,128)(2,1)}, bf16[2,256,512]{2,1,0:T(8,128)(2,1)}, bf16[1,256,512]{2,1,0:T(8,128)(2,1)}, bf16[2,256,512]{2,1,0:T(8,128)(2...) custom-call(s32[1]{0:T(128)} %bitcast.3.refs_0_, ...), custom_call_target="tpu_custom_call" | custom-call | flops 3221225472 | bytes 10485760 | tf_op jit(solution)/shard_map/project/pallas_call | solution.py:216
  97.9 5.8 %collective-permute-start.18 = (bf16[1,256,512]{2,1,0:T(8,128)(2,1)}, bf16[1,256,512]{2,1,0:T(8,128)(2,1)S(1)}, u32[]{:S(2)}, u32[]{:S(2)}) collective-permute-start(bf16[1,256,512]{2,1,0:T(8,128)(2,1)} %get-tuple-element.68), channel_id=1, source_target_pairs={{0,2},{2,0},{4,6},{6,4},{1,3},{3,1},{5,7},{7,5},{8,10},{10,8},{12,... | collective-permute-start | bytes 786440 | tf_op jit(solution)/shard_map/ppermute | solution.py:21
  105.7 5.4 %collective-permute-done.18.refs_3_ = bf16[1,256,512]{2,1,0:T(8,128)(2,1)S(1)} collective-permute-done((bf16[1,256,512]{2,1,0:T(8,128)(2,1)}, bf16[1,256,512]{2,1,0:T(8,128)(2,1)S(1)}, u32[]{:S(2)}, u32[]{:S(2)}) %collective-permute-start.18) | collective-permute-done | bytes 262176 | tf_op jit(solution)/shard_map/ppermute | solution.py:21
  113.9 5.4 %collective-permute-done.19.refs_4_ = bf16[1,256,512]{2,1,0:T(8,128)(2,1)} collective-permute-done((bf16[1,256,512]{2,1,0:T(8,128)(2,1)}, bf16[1,256,512]{2,1,0:T(8,128)(2,1)}, u32[]{:S(2)}, u32[]{:S(2)}) %collective-permute-start.19) | collective-permute-done | bytes 262176 | tf_op jit(solution)/shard_map/ppermute | solution.py:21
  121.6 34.7 %collective-permute-done.20.refs_5_ = bf16[1,256,512]{2,1,0:T(8,128)(2,1)} collective-permute-done((bf16[1,256,512]{2,1,0:T(8,128)(2,1)}, bf16[1,256,512]{2,1,0:T(8,128)(2,1)}, u32[]{:S(2)}, u32[]{:S(2)}) %collective-permute-start.20) | collective-permute-done | bytes 262176 | tf_op jit(solution)/shard_map/ppermute | solution.py:21
  163.3 12.0 %attend.2 = (bf16[1,256,512]{2,1,0:T(8,128)(2,1)}, bf16[1,256,512]{2,1,0:T(8,128)(2,1)}, bf16[1,256,512]{2,1,0:T(8,128)(2,1)}, bf16[1,256,512]{2,1,0:T(8,128)(2,1)}) custom-call(s32[4]{0:T(128)} %slice_bitcast_fusion.24.refs_0_, f32[2,1024,128]{2,1,0:T(8,128)} %pad_maximum_fusion.1.refs_4_.refs_1_, bf16[1,256,512]{2,1,0:T(8,128)(2,1)} %get-tuple-element.67.refs_2_, ...), custom_call_target="tpu_custom_call" | custom-call | flops 4697620480 | bytes 2097152 | tf_op jit(solution)/shard_map/attend/pallas_call | solution.py:299
  175.4 21.3 %attend.3 = (bf16[2,256,512]{2,1,0:T(8,128)(2,1)}, bf16[2,256,512]{2,1,0:T(8,128)(2,1)}, bf16[2,256,512]{2,1,0:T(8,128)(2,1)}, bf16[2,256,512]{2,1,0:T(8,128)(2,1)}) custom-call(s32[8]{0:T(128)} %reshape.329.refs_0_, f32[2,1024,128]{2,1,0:T(8,128)} %pad_maximum_fusion.1.refs_4_.refs_1_, bf16[2,256,512]{2,1,0:T(8,128)(2,1)} %get-tuple-element.72.refs_2_, ...), custom_call_target="tpu_custom_call" | custom-call | flops 9395240960 | bytes 4194304 | tf_op jit(solution)/shard_map/attend/pallas_call | solution.py:299
  204.2 30.6 %feed_forward.1 = (f32[768,1024]{1,0:T(8,128)}, f32[768,1024]{1,0:T(8,128)}, f32[2,256,2048]{2,1,0:T(8,128)}, bf16[2,256,2048]{2,1,0:T(8,128)(2,1)}, f32[2,256,2...) custom-call(bf16[768,1024]{1,0:T(8,128)(2,1)} %get-tuple-element.60.refs_0_, ...), custom_call_target="tpu_custom_call" | custom-call | flops 19327352832 | bytes 46137344 | tf_op jit(solution)/shard_map/feed_forward/pallas_call | solution.py:370
  234.9 5.3 %collective-permute-done.27.refs_12_ = bf16[2,256,512]{2,1,0:T(8,128)(2,1)S(1)} collective-permute-done((bf16[2,256,512]{2,1,0:T(8,128)(2,1)}, bf16[2,256,512]{2,1,0:T(8,128)(2,1)S(1)}, u32[]{:S(2)}, u32[]{:S(2)}) %collective-permute-start.27) | collective-permute-done | bytes 524320 | tf_op jit(solution)/shard_map/ppermute | solution.py:21
  240.2 7.4 %collective-permute-done.29.refs_14_ = bf16[2,256,512]{2,1,0:T(8,128)(2,1)S(1)} collective-permute-done((bf16[2,256,512]{2,1,0:T(8,128)(2,1)}, bf16[2,256,512]{2,1,0:T(8,128)(2,1)S(1)}, u32[]{:S(2)}, u32[]{:S(2)}) %collective-permute-start.29) | collective-permute-done | bytes 524320 | tf_op jit(solution)/shard_map/ppermute | solution.py:21
  248.4 22.8 %finish.1 = (bf16[2,768,1024]{2,1,0:T(8,128)(2,1)}, f32[2,256,1024]{2,1,0:T(8,128)}, bf16[2,256,1024]{2,1,0:T(8,128)(2,1)}, f32[2,256,1024]{2,1,0:T(8,128)}, bf1...) custom-call(s32[1]{0:T(128)} %bitcast.3.refs_0_, bf16[768,1024]{1,0:T(8,128)(2,1)} %get-tuple-element.56.refs_1_, ...), custom_call_target="tpu_custom_call" | custom-call | flops 6442450944 | bytes 32505856 | tf_op jit(solution)/shard_map/finish/pallas_call | solution.py:453
  279.3 18.6 %collective-permute-done.33 = f32[68,128]{1,0:T(8,128)S(1)} collective-permute-done((f32[68,128]{1,0:T(8,128)S(1)}, f32[68,128]{1,0:T(8,128)S(1)}, u32[]{:S(2)}, u32[]{:S(2)}) %collective-permute-start.33) | collective-permute-done | bytes 34848 | tf_op jit(solution)/shard_map/ppermute | solution.py:21
  314.5 46.6 %collective-permute-done.37 = bf16[1,256,1024]{2,1,0:T(8,128)(2,1)S(1)} collective-permute-done((bf16[1,256,1024]{2,1,0:T(8,128)(2,1)S(1)}, bf16[1,256,1024]{2,1,0:T(8,128)(2,1)S(1)}, u32[]{:S(2)}, u32[]{:S(2)}) %collective-permute-start.37) | collective-permute-done | bytes 524320 | tf_op jit(solution)/shard_map/ppermute | solution.py:21
  387.1 5.2 %collective-permute-done.44 = bf16[1,256,2048]{2,1,0:T(8,128)(2,1)} collective-permute-done((bf16[1,256,2048]{2,1,0:T(8,128)(2,1)S(1)}, bf16[1,256,2048]{2,1,0:T(8,128)(2,1)}, u32[]{:S(2)}, u32[]{:S(2)}) %collective-permute-start.44) | collective-permute-done | bytes 1048608 | tf_op jit(solution)/shard_map/ppermute | solution.py:21
  404.9 7.7 %close.1 = (bf16[768,1024]{1,0:T(8,128)(2,1)}, bf16[768,1024]{1,0:T(8,128)(2,1)}) custom-call(s32[1]{0:T(128)} %bitcast.refs_0_, bf16[768,1024]{1,0:T(8,128)(2,1)} %get-tuple-element.56.refs_1_, bf16[768,1024]{1,0:T(8,128)(2,1)} %get-tuple-element.57.refs_1_.refs_3_.refs_2_, bf16[2,768,1024]{2,1,0:T(8,128)(2,1)} %get-tuple-element.83.refs_3_, ...), custom_call_target="tpu_custom_call" | custom-call | flops 23592960 | bytes 12582912 | tf_op jit(solution)/shard_map/close/pallas_call | solution.py:498
  412.6 6.0 %collective-permute-done.47 = bf16[64,4096]{1,0:T(8,128)(2,1)S(1)} collective-permute-done((bf16[64,4096]{1,0:T(8,128)(2,1)S(1)}, bf16[64,4096]{1,0:T(8,128)(2,1)S(1)}, u32[]{:S(2)}, u32[]{:S(2)}) %collective-permute-start.47) | collective-permute-done | bytes 524320 | tf_op jit(solution)/shard_map/ppermute | solution.py:21
  418.6 18.9 %collective-permute-done.48 = bf16[64,4096]{1,0:T(8,128)(2,1)S(1)} collective-permute-done((bf16[64,4096]{1,0:T(8,128)(2,1)S(1)}, bf16[64,4096]{1,0:T(8,128)(2,1)S(1)}, u32[]{:S(2)}, u32[]{:S(2)}) %collective-permute-start.48) | collective-permute-done | bytes 524320 | tf_op jit(solution)/shard_map/ppermute | solution.py:21
  437.4 7.2 %collective-permute-done.49 = bf16[64,4096]{1,0:T(8,128)(2,1)S(1)} collective-permute-done((bf16[64,4096]{1,0:T(8,128)(2,1)S(1)}, bf16[64,4096]{1,0:T(8,128)(2,1)S(1)}, u32[]{:S(2)}, u32[]{:S(2)}) %collective-permute-start.49) | collective-permute-done | bytes 524320 | tf_op jit(solution)/shard_map/ppermute | solution.py:21
  (266 shorter events, 116.4 us)
Async XLA Ops:
  28.8 37.9 %collective-permute-start.4 = (bf16[64,4096]{1,0:T(8,128)(2,1)S(1)}, bf16[64,4096]{1,0:T(8,128)(2,1)S(1)}, u32[]{:S(2)}, u32[]{:S(2)}) collective-permute-start(bf16[64,4096]{1,0:T(8,128)(2,1)S(1)} %pad_maximum_fusion.2), channel_id=1, source_target_pairs={{0,4},{2,6},{4,0},{6,2},{1,5},{3,7},{5,1},{7,3},{8,12},{10,14},{12... | collective-permute-start | bytes 1572872 | tf_op jit(solution)/shard_map/ppermute | solution.py:21
  32.5 36.2 %collective-permute-start.16 = (bf16[256,1024]{1,0:T(8,128)(2,1)S(1)}, bf16[256,1024]{1,0:T(8,128)(2,1)S(1)}, u32[]{:S(2)}, u32[]{:S(2)}) collective-permute-start(bf16[256,1024]{1,0:T(8,128)(2,1)S(1)} %get-tuple-element.158.refs_10_.refs_19_), channel_id=1, source_target_pairs={{0,16},{8,24},{16,0},{24,8},{1,17},{9,25},{17,1},{25,9},{2,18},{10... | collective-permute-start | bytes 1572872 | tf_op jit(solution)/shard_map/ppermute | solution.py:21
  34.1 42.2 %collective-permute-start.5 = (bf16[64,4096]{1,0:T(8,128)(2,1)S(1)}, bf16[64,4096]{1,0:T(8,128)(2,1)S(1)}, u32[]{:S(2)}, u32[]{:S(2)}) collective-permute-start(bf16[64,4096]{1,0:T(8,128)(2,1)S(1)} %pad_maximum_fusion.2), channel_id=1, source_target_pairs={{0,6},{2,4},{4,2},{6,0},{1,7},{3,5},{5,3},{7,1},{8,14},{10,12},{12... | collective-permute-start | bytes 1572872 | tf_op jit(solution)/shard_map/ppermute | solution.py:21
  76.5 82.6 %collective-permute-start.10 = (bf16[256,2048]{1,0:T(8,128)(2,1)S(1)}, bf16[256,2048]{1,0:T(8,128)(2,1)S(1)}, u32[]{:S(2)}, u32[]{:S(2)}) collective-permute-start(bf16[256,2048]{1,0:T(8,128)(2,1)S(1)} %get-tuple-element.148.refs_9_), channel_id=1, source_target_pairs={{0,16},{8,24},{16,0},{24,8},{1,17},{9,25},{17,1},{25,9},{2,18},{10... | collective-permute-start | bytes 3145736 | tf_op jit(solution)/shard_map/ppermute | solution.py:21
  78.1 81.9 %collective-permute-start.6 = (bf16[256,2048]{1,0:T(8,128)(2,1)S(1)}, bf16[256,2048]{1,0:T(8,128)(2,1)}, u32[]{:S(2)}, u32[]{:S(2)}) collective-permute-start(bf16[256,2048]{1,0:T(8,128)(2,1)S(1)} %get-tuple-element.149.refs_5_), channel_id=1, source_target_pairs={{0,8},{8,0},{16,24},{24,16},{1,9},{9,1},{17,25},{25,17},{2,10},{10... | collective-permute-start | bytes 3145736 | tf_op jit(solution)/shard_map/ppermute | solution.py:21
  103.7 57.4 %collective-permute-start.21 = (bf16[2,256,512]{2,1,0:T(8,128)(2,1)}, bf16[2,256,512]{2,1,0:T(8,128)(2,1)}, u32[]{:S(2)}, u32[]{:S(2)}) collective-permute-start(bf16[2,256,512]{2,1,0:T(8,128)(2,1)} %get-tuple-element.73), channel_id=1, source_target_pairs={{0,2},{2,0},{4,6},{6,4},{1,3},{3,1},{5,7},{7,5},{8,10},{10,8},{12,... | collective-permute-start | bytes 1572872 | tf_op jit(solution)/shard_map/ppermute | solution.py:21
  111.1 50.9 %collective-permute-start.22 = (bf16[2,256,512]{2,1,0:T(8,128)(2,1)}, bf16[2,256,512]{2,1,0:T(8,128)(2,1)}, u32[]{:S(2)}, u32[]{:S(2)}) collective-permute-start(bf16[2,256,512]{2,1,0:T(8,128)(2,1)} %get-tuple-element.74), channel_id=1, source_target_pairs={{0,4},{2,6},{4,0},{6,2},{1,5},{3,7},{5,1},{7,3},{8,12},{10,14},{12... | collective-permute-start | bytes 1572872 | tf_op jit(solution)/shard_map/ppermute | solution.py:21
  119.3 37.0 %collective-permute-start.20 = (bf16[1,256,512]{2,1,0:T(8,128)(2,1)}, bf16[1,256,512]{2,1,0:T(8,128)(2,1)}, u32[]{:S(2)}, u32[]{:S(2)}) collective-permute-start(bf16[1,256,512]{2,1,0:T(8,128)(2,1)} %get-tuple-element.70), channel_id=1, source_target_pairs={{0,6},{2,4},{4,2},{6,0},{1,7},{3,5},{5,3},{7,1},{8,14},{10,12},{12... | collective-permute-start | bytes 786440 | tf_op jit(solution)/shard_map/ppermute | solution.py:21
  159.1 37.5 %collective-permute-start.7 = (bf16[256,2048]{1,0:T(8,128)(2,1)S(1)}, bf16[256,2048]{1,0:T(8,128)(2,1)S(1)}, u32[]{:S(2)}, u32[]{:S(2)}) collective-permute-start(bf16[256,2048]{1,0:T(8,128)(2,1)S(1)} %get-tuple-element.149.refs_5_), channel_id=1, source_target_pairs={{0,16},{8,24},{16,0},{24,8},{1,17},{9,25},{17,1},{25,9},{2,18},{10... | collective-permute-start | bytes 3145736 | tf_op jit(solution)/shard_map/ppermute | solution.py:21
  160.0 39.8 %collective-permute-start.9 = (bf16[256,2048]{1,0:T(8,128)(2,1)S(1)}, bf16[256,2048]{1,0:T(8,128)(2,1)S(1)}, u32[]{:S(2)}, u32[]{:S(2)}) collective-permute-start(bf16[256,2048]{1,0:T(8,128)(2,1)S(1)} %get-tuple-element.148.refs_9_), channel_id=1, source_target_pairs={{0,8},{8,0},{16,24},{24,16},{1,9},{9,1},{17,25},{25,17},{2,10},{10... | collective-permute-start | bytes 3145736 | tf_op jit(solution)/shard_map/ppermute | solution.py:21
  161.2 40.1 %collective-permute-start.11 = (bf16[256,2048]{1,0:T(8,128)(2,1)S(1)}, bf16[256,2048]{1,0:T(8,128)(2,1)S(1)}, u32[]{:S(2)}, u32[]{:S(2)}) collective-permute-start(bf16[256,2048]{1,0:T(8,128)(2,1)S(1)} %collective-permute-done.10.refs_11_), channel_id=1, source_target_pairs={{0,8},{8,0},{16,24},{24,16},{1,9},{9,1},{17,25},{25,17},{2,10},{10... | collective-permute-start | bytes 3145736 | tf_op jit(solution)/shard_map/ppermute | solution.py:21
  162.0 41.3 %collective-permute-start.8 = (bf16[256,2048]{1,0:T(8,128)(2,1)}, bf16[256,2048]{1,0:T(8,128)(2,1)S(1)}, u32[]{:S(2)}, u32[]{:S(2)}) collective-permute-start(bf16[256,2048]{1,0:T(8,128)(2,1)} %collective-permute-done.6.refs_6_), channel_id=1, source_target_pairs={{0,16},{8,24},{16,0},{24,8},{1,17},{9,25},{17,1},{25,9},{2,18},{10... | collective-permute-start | bytes 3145736 | tf_op jit(solution)/shard_map/ppermute | solution.py:21
  196.6 38.2 %collective-permute-start.26 = (bf16[1,256,512]{2,1,0:T(8,128)(2,1)}, bf16[1,256,512]{2,1,0:T(8,128)(2,1)S(1)}, u32[]{:S(2)}, u32[]{:S(2)}) collective-permute-start(bf16[1,256,512]{2,1,0:T(8,128)(2,1)} %get-tuple-element.79), channel_id=1, source_target_pairs={{0,4},{2,6},{4,0},{6,2},{1,5},{3,7},{5,1},{7,3},{8,12},{10,14},{12... | collective-permute-start | bytes 786440 | tf_op jit(solution)/shard_map/ppermute | solution.py:21
  201.3 38.9 %collective-permute-start.27 = (bf16[2,256,512]{2,1,0:T(8,128)(2,1)}, bf16[2,256,512]{2,1,0:T(8,128)(2,1)S(1)}, u32[]{:S(2)}, u32[]{:S(2)}) collective-permute-start(bf16[2,256,512]{2,1,0:T(8,128)(2,1)} %get-tuple-element.80), channel_id=1, source_target_pairs={{0,4},{2,6},{4,0},{6,2},{1,5},{3,7},{5,1},{7,3},{8,12},{10,14},{12... | collective-permute-start | bytes 1572872 | tf_op jit(solution)/shard_map/ppermute | solution.py:21
  203.3 44.4 %collective-permute-start.29 = (bf16[2,256,512]{2,1,0:T(8,128)(2,1)}, bf16[2,256,512]{2,1,0:T(8,128)(2,1)S(1)}, u32[]{:S(2)}, u32[]{:S(2)}) collective-permute-start(bf16[2,256,512]{2,1,0:T(8,128)(2,1)} %get-tuple-element.82), channel_id=1, source_target_pairs={{0,6},{2,4},{4,2},{6,0},{1,7},{3,5},{5,3},{7,1},{8,14},{10,12},{12... | collective-permute-start | bytes 1572872 | tf_op jit(solution)/shard_map/ppermute | solution.py:21
  271.4 35.5 %collective-permute-start.36 = (bf16[2,256,1024]{2,1,0:T(8,128)(2,1)}, bf16[2,256,1024]{2,1,0:T(8,128)(2,1)S(1)}, u32[]{:S(2)}, u32[]{:S(2)}) collective-permute-start(bf16[2,256,1024]{2,1,0:T(8,128)(2,1)} %get-tuple-element.91), channel_id=1, source_target_pairs={{0,16},{8,24},{16,0},{24,8},{1,17},{9,25},{17,1},{25,9},{2,18},{10... | collective-permute-start | bytes 3145736 | tf_op jit(solution)/shard_map/ppermute | solution.py:21
  275.3 36.0 %collective-permute-start.38 = (bf16[2,256,1024]{2,1,0:T(8,128)(2,1)}, bf16[2,256,1024]{2,1,0:T(8,128)(2,1)}, u32[]{:S(2)}, u32[]{:S(2)}) collective-permute-start(bf16[2,256,1024]{2,1,0:T(8,128)(2,1)} %get-tuple-element.93), channel_id=1, source_target_pairs={{0,8},{8,0},{16,24},{24,16},{1,9},{9,1},{17,25},{25,17},{2,10},{10... | collective-permute-start | bytes 3145736 | tf_op jit(solution)/shard_map/ppermute | solution.py:21
  302.6 62.1 %collective-permute-start.43 = (bf16[2,256,2048]{2,1,0:T(8,128)(2,1)}, bf16[2,256,2048]{2,1,0:T(8,128)(2,1)}, u32[]{:S(2)}, u32[]{:S(2)}) collective-permute-start(bf16[2,256,2048]{2,1,0:T(8,128)(2,1)} %get-tuple-element.95), channel_id=1, source_target_pairs={{0,16},{8,24},{16,0},{24,8},{1,17},{9,25},{17,1},{25,9},{2,18},{10... | collective-permute-start | bytes 6291464 | tf_op jit(solution)/shard_map/ppermute | solution.py:21
  303.4 66.8 %collective-permute-start.45 = (bf16[2,256,2048]{2,1,0:T(8,128)(2,1)}, bf16[2,256,2048]{2,1,0:T(8,128)(2,1)}, u32[]{:S(2)}, u32[]{:S(2)}) collective-permute-start(bf16[2,256,2048]{2,1,0:T(8,128)(2,1)} %get-tuple-element.97), channel_id=1, source_target_pairs={{0,8},{8,0},{16,24},{24,16},{1,9},{9,1},{17,25},{25,17},{2,10},{10... | collective-permute-start | bytes 6291464 | tf_op jit(solution)/shard_map/ppermute | solution.py:21
  306.8 98.1 %collective-permute-start.30 = (bf16[2,768,1024]{2,1,0:T(8,128)(2,1)}, bf16[2,768,1024]{2,1,0:T(8,128)(2,1)}, u32[]{:S(2)}, u32[]{:S(2)}) collective-permute-start(bf16[2,768,1024]{2,1,0:T(8,128)(2,1)} %get-tuple-element.83.refs_3_), channel_id=1, source_target_pairs={{0,1},{1,0},{2,3},{3,2},{4,5},{5,4},{6,7},{7,6},{8,9},{9,8},{10,11... | collective-permute-start | bytes 9437192 | tf_op jit(solution)/shard_map/ppermute | solution.py:21
  308.5 52.6 %collective-permute-start.37 = (bf16[1,256,1024]{2,1,0:T(8,128)(2,1)S(1)}, bf16[1,256,1024]{2,1,0:T(8,128)(2,1)S(1)}, u32[]{:S(2)}, u32[]{:S(2)}) collective-permute-start(bf16[1,256,1024]{2,1,0:T(8,128)(2,1)S(1)} %fusion.6), channel_id=1, source_target_pairs={{0,8},{8,0},{16,24},{24,16},{1,9},{9,1},{17,25},{25,17},{2,10},{10... | collective-permute-start | bytes 1572872 | tf_op jit(solution)/shard_map/ppermute | solution.py:21
  313.3 48.1 %collective-permute-start.39 = (bf16[1,256,1024]{2,1,0:T(8,128)(2,1)S(1)}, bf16[1,256,1024]{2,1,0:T(8,128)(2,1)S(1)}, u32[]{:S(2)}, u32[]{:S(2)}) collective-permute-start(bf16[1,256,1024]{2,1,0:T(8,128)(2,1)S(1)} %fusion.4), channel_id=1, source_target_pairs={{0,16},{8,24},{16,0},{24,8},{1,17},{9,25},{17,1},{25,9},{2,18},{10... | collective-permute-start | bytes 1572872 | tf_op jit(solution)/shard_map/ppermute | solution.py:21
  401.7 35.7 %collective-permute-start.48 = (bf16[64,4096]{1,0:T(8,128)(2,1)S(1)}, bf16[64,4096]{1,0:T(8,128)(2,1)S(1)}, u32[]{:S(2)}, u32[]{:S(2)}) collective-permute-start(bf16[64,4096]{1,0:T(8,128)(2,1)S(1)} %pad_maximum_fusion.4), channel_id=1, source_target_pairs={{0,4},{2,6},{4,0},{6,2},{1,5},{3,7},{5,1},{7,3},{8,12},{10,14},{12... | collective-permute-start | bytes 1572872 | tf_op jit(solution)/shard_map/ppermute | solution.py:21
  402.8 41.8 %collective-permute-start.49 = (bf16[64,4096]{1,0:T(8,128)(2,1)S(1)}, bf16[64,4096]{1,0:T(8,128)(2,1)S(1)}, u32[]{:S(2)}, u32[]{:S(2)}) collective-permute-start(bf16[64,4096]{1,0:T(8,128)(2,1)S(1)} %pad_maximum_fusion.5), channel_id=1, source_target_pairs={{0,6},{2,4},{4,2},{6,0},{1,7},{3,5},{5,3},{7,1},{8,14},{10,12},{12... | collective-permute-start | bytes 1572872 | tf_op jit(solution)/shard_map/ppermute | solution.py:21
  (70 other events, 1421.9 us)
